TPU v7x, 128 devices: a whole 4x4x4 slice. The times are simulated.
128 devices in a mesh: elem: 128 (over x, y, z, core).
Axes of the slice: x: 4, y: 4, z: 4, core: 2. Of those that a mesh axis runs over, the one named last changes fastest.
Arguments:
- elem_mats: bfloat16 [1536, 750, 750], P('elem'), may hold values from -0.14 to 0.64
- face_blocks: bfloat16 [3456, 125, 125], P('elem'), may hold values from -0.45 to 1.25
- rhs: bfloat16 [3456, 16, 125], P('elem'), may hold values from -6 to 6
- elem_faces: int32 [1536, 6], replicated, may hold values from 0 to 3455, as said below
- orient: int32 [1536, 6], replicated, may hold values from 0 to 7
- counts: int32 [128], replicated, may hold values from 3 to 9, as said below
Outputs:
- traces: float32 [3456, 16, 125], P('elem')
Inputs may be any that keep to these rules, and one draw needn't show every extreme that they name: Element slots 0 to counts[d] - 1 of device d (rows d * 12 onward) are live, the others empty; counts[2 i] + counts[2 i + 1] = 12. `elem_faces`: face f is owned by device f // 27. A live element slot of device d has all its faces owned by devices d - 2 to d + 2; device d has exactly 4 live element faces owned by each other device within that distance; a face is listed by at most two live element faces. Rows of empty slots hold arbitrary faces.
All inputs are finite; a program needn't handle non-finite values.
Results may differ from a plain program's by a relative error of at most 0.0017.
Values may be sent and summed in bfloat16 or wider, within the bound.
A program may use at most 128 MiB of HBM per device.

v0:
```python
import jax
import jax.numpy as jnp
import numpy as np
from jax import lax
from jax.sharding import PartitionSpec as P

COMP = 5
EDGE = 5
ITERS = 2
REACH = 2
SLOT = 4


def passed_along(block, axis, distance):
    devices = range(lax.axis_size(axis))
    route = [(i - distance, i) for i in devices if i - distance in devices]
    return lax.ppermute(block, axis, route)


def orient_tables(edge_nodes, components):
    node_ids = np.arange(edge_nodes * edge_nodes)
    row_pos = node_ids // edge_nodes
    col_pos = node_ids % edge_nodes
    table_rows = []
    for orient_code in range(8):
        if orient_code & 4:
            first_pos, second_pos = (col_pos, row_pos)
        else:
            first_pos, second_pos = (row_pos, col_pos)
        if orient_code & 1:
            first_pos = edge_nodes - 1 - first_pos
        if orient_code & 2:
            second_pos = edge_nodes - 1 - second_pos
        moved_node = first_pos * edge_nodes + second_pos
        table_rows.append(
            np.concatenate(
                [
                    part_index * edge_nodes * edge_nodes + moved_node
                    for part_index in range(components)
                ]
            )
        )
    forward = np.stack(table_rows).astype(np.int32)
    backward = np.argsort(forward, axis=1).astype(np.int32)
    return (forward, backward)


def face_offsets():
    return [step_size for step_size in range(1, REACH + 1)] + [
        -step_size for step_size in range(1, REACH + 1)
    ]


def pick_slots(chosen, values):
    rank_in = jnp.cumsum(chosen.astype(jnp.int32)) - 1
    slot_ids = jnp.arange(SLOT, dtype=jnp.int32)
    matches = chosen[None, :] & (rank_in[None, :] == slot_ids[:, None])
    present = jnp.any(matches, axis=1)
    picked = jnp.sum(jnp.where(matches, values[None, :], 0), axis=1)
    return (picked, present, rank_in)


def device_rows(elem_faces, counts, device, elem_cap, face_dev):
    devices_all = counts.shape[0]
    safe_device = jnp.clip(device, 0, devices_all - 1)
    faces_here = lax.dynamic_slice_in_dim(elem_faces, safe_device * elem_cap, elem_cap, 0).reshape(
        -1
    )
    slot_elem = jnp.arange(elem_cap * 6, dtype=jnp.int32) // 6
    is_live = (slot_elem < counts[safe_device]) & (device >= 0) & (device < devices_all)
    return (faces_here // face_dev, faces_here % face_dev, is_live)


def move_direct(piece, step_by, back):
    if back:
        return passed_along(piece, "elem", step_by)
    return passed_along(piece, "elem", step_by)


def deliver(pieces, back):
    offsets = face_offsets()
    results = []
    for offset, piece in zip(offsets, pieces):
        results.append(move_direct(piece, -offset if back else offset, back))
    return results


def element_terms(elem_frame, matrices, trace_len):
    blocks = matrices.reshape(matrices.shape[0], 6, trace_len, 6, trace_len)
    return jnp.einsum("akni,akilj->alnj", elem_frame, blocks, preferred_element_type=jnp.float32)


def per_device(elem_mats, face_blocks, rhs, elem_faces, orient, counts):
    my_index = lax.axis_index("elem")
    elem_cap = elem_mats.shape[0]
    face_dev = face_blocks.shape[0]
    trace_len = face_blocks.shape[1]
    functionals = rhs.shape[1]
    top_live = elem_cap - elem_cap // 4
    incidences = elem_cap * 6
    forward, backward = orient_tables(EDGE, COMP)
    my_orient = lax.dynamic_slice_in_dim(orient, my_index * elem_cap, elem_cap, 0).reshape(-1)
    to_element = jnp.asarray(forward)[my_orient]
    to_face = jnp.asarray(backward)[my_orient]
    owners, local_faces, is_live = device_rows(elem_faces, counts, my_index, elem_cap, face_dev)
    offsets = face_offsets()
    at_home = is_live & (owners == my_index)
    table_index = jnp.where(at_home, local_faces, 0)
    home_ids = jnp.where(at_home, local_faces, face_dev)
    send_picks = []
    send_present = []
    for group_index, offset in enumerate(offsets):
        chosen = is_live & (owners == my_index + offset)
        picked, present, rank_in = pick_slots(chosen, jnp.arange(incidences, dtype=jnp.int32))
        send_picks.append(picked)
        send_present.append(present)
        table_index = jnp.where(chosen, face_dev + group_index * SLOT + rank_in, table_index)
    recv_faces = []
    for offset in offsets:
        src_owners, src_local, src_live = device_rows(
            elem_faces, counts, my_index - offset, elem_cap, face_dev
        )
        chosen = src_live & (src_owners == my_index)
        picked, present, rank_in = pick_slots(chosen, src_local)
        recv_faces.append(jnp.where(present, picked, face_dev))
    my_count = counts[my_index]
    live_rows = jnp.arange(elem_cap, dtype=jnp.int32) < my_count
    traces = jnp.zeros((face_dev, functionals, trace_len), jnp.float32)
    for sweep_index in range(ITERS):
        rounded = traces.astype(jnp.bfloat16)
        back_buckets = [rounded[jnp.clip(face_ids, 0, face_dev - 1)] for face_ids in recv_faces]
        returned = deliver(back_buckets, True)
        source_table = jnp.concatenate([rounded] + returned, axis=0)
        gathered = source_table[table_index]
        elem_frame = jnp.take_along_axis(gathered, to_element[:, None, :], axis=2).reshape(
            elem_cap, 6, functionals, trace_len
        )
        upper_terms = element_terms(elem_frame[:top_live], elem_mats[:top_live], trace_len).astype(
            jnp.bfloat16
        )
        padding = jnp.zeros((elem_cap - top_live,) + upper_terms.shape[1:], jnp.bfloat16)
        elem_terms = jnp.concatenate([upper_terms, padding], axis=0)
        elem_terms = jnp.where(
            live_rows[:, None, None, None], elem_terms, jnp.zeros_like(elem_terms)
        )
        face_terms = jnp.take_along_axis(
            elem_terms.reshape(incidences, functionals, trace_len), to_face[:, None, :], axis=2
        )
        buckets = []
        for picked, present in zip(send_picks, send_present):
            chosen_rows = face_terms[picked]
            buckets.append(
                jnp.where(present[:, None, None], chosen_rows, jnp.zeros_like(chosen_rows))
            )
        arrived = deliver(buckets, False)
        summed = jax.ops.segment_sum(
            face_terms.astype(jnp.float32), home_ids, num_segments=face_dev
        )
        for face_ids, arrived_piece in zip(recv_faces, arrived):
            summed = summed + jax.ops.segment_sum(
                arrived_piece.astype(jnp.float32), face_ids, num_segments=face_dev
            )
        residual = (rhs.astype(jnp.float32) - summed).astype(jnp.bfloat16)
        traces = traces + jnp.einsum(
            "fni,fij->fnj", residual, face_blocks, preferred_element_type=jnp.float32
        )
    return traces


def solution(mesh):
    in_specs = (P("elem", None, None), P("elem", None, None), P("elem", None, None), P(), P(), P())
    out_specs = P("elem", None, None)
    return jax.shard_map(
        per_device, mesh=mesh, in_specs=in_specs, out_specs=out_specs, check_vma=False
    )
```

profile of v0, /device:TPU:6, one launch (start us, length us, event | category | flops | bytes accessed | tf_op | source)
XLA Modules:
  0.0 566.7 jit_solution(16256493660898159520)
XLA Ops:
  0.0 1.0 compare_and_fusion.6
  1.0 1.0 dynamic-slice_divide_fusion
  2.7 1.6 fusion.78
  9.2 1.9 collective-permute-start.2
  16.8 8.7 %collective-permute-start.1 = (bf16[4,16,125]{2,1,0:T(8,128)(2,1)S(1)}, bf16[4,16,125]{2,1,0:T(8,128)(2,1)S(1)}, u32[]{:S(2)}, u32[]{:S(2)}) collective-permute-start(bf16[4,16,125]{2,1,0:T(8,128)(2,1)S(1)} %gather_fusion.1), channel_id=1, source_target_pairs={{2,0},{3,1},{4,2},{5,3},{6,4},{7,5},{8,6},{9,7},{10,8},{11,9},{12,... | collective-permute-start | bytes 48008 | tf_op jit(solution)/shard_map/ppermute | solution.py:17
  26.2 3.4 collective-permute-start
  30.2 1.9 collective-permute-start.3
  33.3 1.3 gather_fusion.5
  34.6 1.3 gather_fusion.6
  41.4 8.5 %slice.18 = bf16[9,750,750]{2,1,0:T(8,128)(2,1)} slice(bf16[12,750,750]{2,1,0:T(8,128)(2,1)} %param.10), slice={[0:9], [0:750], [0:750]} | slice | bytes 20250000 | tf_op jit(solution)/shard_map/slice | solution.py:138
  49.9 17.1 %reshape.1200 = bf16[9,6,125,6,125]{4,3,2,1,0:T(8,128)(2,1)} reshape(bf16[9,750,750]{2,1,0:T(8,128)(2,1)} %slice.18) | data formatting | bytes 20250000 | tf_op jit(solution)/shard_map/reshape | solution.py:89
  67.2 1.3 gather_fusion.4
  68.6 2.6 copy.238
  71.2 97.9 %gather_fusion.20 = bf16[9000,16]{1,0:T(8,128)(2,1)} fusion(bf16[72,16,125]{1,0,2:T(8,128)(2,1)S(1)} %copy.238, s32[9000]{0:T(1024)S(1)} %reshape.1464), kind=kCustom, calls=%fused_computation.clone | custom fusion | bytes 648000 | tf_op jit(solution)/shard_map/jit(take_along_axis)/gather | solution.py:135
  169.0 2.2 copy.239
  171.7 6.5 %fusion.16 = bf16[9,6,16,125]{3,2,1,0:T(8,128)(2,1)S(1)} fusion(bf16[9,6,16,125,1]{3,2,1,4,0:T(8,128)(2,1)S(1)} %bitcast.124, bf16[9,6,125,6,125]{4,3,2,1,0:T(8,128)(2,1)} %reshape.1200), kind=kOutput, calls=%fused_computation.39 | convolution fusion | flops 162108000 | bytes 10557000 | tf_op jit(solution)/shard_map/akni,akilj->alnj/dot_general | solution.py:90
  178.2 0.8 pad_select_fusion.1
  179.0 2.6 copy.242
  181.6 97.9 %gather_fusion.21 = bf16[9000,16]{1,0:T(8,128)(2,1)} fusion(bf16[72,16,125]{1,0,2:T(8,128)(2,1)S(1)} %copy.242, s32[9000]{0:T(1024)S(1)} %reshape.1469), kind=kCustom, calls=%fused_computation.1.clone | custom fusion | bytes 648000 | tf_op jit(solution)/shard_map/jit(take_along_axis)/gather | solution.py:146
  279.4 2.2 copy.243
  282.8 1.9 collective-permute-start.5
  285.4 6.5 %collective-permute-start.6 = (bf16[4,16,125]{2,1,0:T(8,128)(2,1)S(1)}, bf16[4,16,125]{2,1,0:T(8,128)(2,1)S(1)}, u32[]{:S(2)}, u32[]{:S(2)}) collective-permute-start(bf16[4,16,125]{2,1,0:T(8,128)(2,1)S(1)} %broadcast_select_fusion.3), channel_id=1, source_target_pairs={{1,0},{2,1},{3,2},{4,3},{5,4},{6,5},{7,6},{8,7},{9,8},{10,9},{11,1... | collective-permute-start | bytes 48008 | tf_op jit(solution)/shard_map/ppermute | solution.py:17
  292.5 3.6 collective-permute-start.7
  296.8 2.0 collective-permute-start.4
  299.0 3.7 scatter_fusion
  302.6 3.4 collective-permute-done.4
  306.9 1.0 scatter_fusion.2
  307.9 1.0 constant_dynamic-update-slice_fusion.8
  309.5 4.5 collective-permute-start.8
  315.7 1.9 collective-permute-start.11
  317.7 1.9 collective-permute-start.10
  319.6 8.1 %collective-permute-start.9 = (bf16[4,16,125]{2,1,0:T(8,128)(2,1)S(1)}, bf16[4,16,125]{2,1,0:T(8,128)(2,1)S(1)}, u32[]{:S(2)}, u32[]{:S(2)}) collective-permute-start(bf16[4,16,125]{2,1,0:T(8,128)(2,1)S(1)} %gather_fusion.12), channel_id=1, source_target_pairs={{2,0},{3,1},{4,2},{5,3},{6,4},{7,5},{8,6},{9,7},{10,8},{11,9},{12,... | collective-permute-start | bytes 48008 | tf_op jit(solution)/shard_map/ppermute | solution.py:17
  327.8 1.4 collective-permute-done.9
  329.2 1.3 gather_fusion.15
  330.5 2.6 copy.247
  333.1 97.9 %gather_fusion.22 = bf16[9000,16]{1,0:T(8,128)(2,1)} fusion(bf16[72,16,125]{1,0,2:T(8,128)(2,1)S(1)} %copy.247, s32[9000]{0:T(1024)S(1)} %reshape.1464), kind=kCustom, calls=%fused_computation.2.clone | custom fusion | bytes 648000 | tf_op jit(solution)/shard_map/jit(take_along_axis)/gather | solution.py:135
  431.0 2.2 copy.248
  433.7 6.5 %fusion.19 = bf16[9,6,16,125]{3,2,1,0:T(8,128)(2,1)S(1)} fusion(bf16[9,6,16,125,1]{3,2,1,4,0:T(8,128)(2,1)S(1)} %bitcast.123, bf16[9,6,125,6,125]{4,3,2,1,0:T(8,128)(2,1)} %reshape.1200), kind=kOutput, calls=%fused_computation.40 | convolution fusion | flops 162108000 | bytes 10557000 | tf_op jit(solution)/shard_map/akni,akilj->alnj/dot_general | solution.py:90
  440.3 1.8 copy.251
  442.2 97.9 %gather_fusion.23 = bf16[9000,16]{1,0:T(8,128)(2,1)} fusion(bf16[72,16,125]{1,0,2:T(8,128)(2,1)S(1)} %copy.251, s32[9000]{0:T(1024)S(1)} %reshape.1469), kind=kCustom, calls=%fused_computation.3.clone | custom fusion | bytes 648000 | tf_op jit(solution)/shard_map/jit(take_along_axis)/gather | solution.py:146
  540.1 2.2 copy.252
  545.1 1.9 collective-permute-start.13
  547.1 7.0 %collective-permute-start.14 = (bf16[4,16,125]{2,1,0:T(8,128)(2,1)S(1)}, bf16[4,16,125]{2,1,0:T(8,128)(2,1)S(1)}, u32[]{:S(2)}, u32[]{:S(2)}) collective-permute-start(bf16[4,16,125]{2,1,0:T(8,128)(2,1)S(1)} %broadcast_select_fusion.2), channel_id=1, source_target_pairs={{1,0},{2,1},{3,2},{4,3},{5,4},{6,5},{7,6},{8,7},{9,8},{10,9},{11,1... | collective-permute-start | bytes 48008 | tf_op jit(solution)/shard_map/ppermute | solution.py:17
  554.2 1.9 collective-permute-start.12
  556.2 3.8 collective-permute-start.15
  560.1 3.7 scatter_fusion.3
  564.6 1.0 scatter_fusion.5
  565.6 1.1 convolution_add_fusion
  (225 shorter events, 30.1 us)
Async XLA Ops:
  0.0 307.9 %copy-start = (bf16[27,125,125]{2,1,0:T(8,128)(2,1)S(1)}, bf16[27,125,125]{2,1,0:T(8,128)(2,1)}, u32[]{:S(2)}) copy-start(bf16[27,125,125]{2,1,0:T(8,128)(2,1)} %param.11) | copy-start | bytes 2531254
  9.2 58.0 %collective-permute-start.2 = (bf16[4,16,125]{2,1,0:T(8,128)(2,1)S(1)}, bf16[4,16,125]{2,1,0:T(8,128)(2,1)S(1)}, u32[]{:S(2)}, u32[]{:S(2)}) collective-permute-start(bf16[4,16,125]{2,1,0:T(8,128)(2,1)S(1)} %gather_fusion.2), channel_id=1, source_target_pairs={{0,1},{1,2},{2,3},{3,4},{4,5},{5,6},{6,7},{7,8},{8,9},{9,10},{10,1... | collective-permute-start | bytes 48008 | tf_op jit(solution)/shard_map/ppermute | solution.py:17
  16.8 50.3 %collective-permute-start.1 = (bf16[4,16,125]{2,1,0:T(8,128)(2,1)S(1)}, bf16[4,16,125]{2,1,0:T(8,128)(2,1)S(1)}, u32[]{:S(2)}, u32[]{:S(2)}) collective-permute-start(bf16[4,16,125]{2,1,0:T(8,128)(2,1)S(1)} %gather_fusion.1), channel_id=1, source_target_pairs={{2,0},{3,1},{4,2},{5,3},{6,4},{7,5},{8,6},{9,7},{10,8},{11,9},{12,... | collective-permute-start | bytes 48008 | tf_op jit(solution)/shard_map/ppermute | solution.py:17
  26.2 41.0 %collective-permute-start = (bf16[4,16,125]{2,1,0:T(8,128)(2,1)S(1)}, bf16[4,16,125]{2,1,0:T(8,128)(2,1)S(1)}, u32[]{:S(2)}, u32[]{:S(2)}) collective-permute-start(bf16[4,16,125]{2,1,0:T(8,128)(2,1)S(1)} %gather_fusion), channel_id=1, source_target_pairs={{1,0},{2,1},{3,2},{4,3},{5,4},{6,5},{7,6},{8,7},{9,8},{10,9},{11,1... | collective-permute-start | bytes 48008 | tf_op jit(solution)/shard_map/ppermute | solution.py:17
  30.2 36.9 %collective-permute-start.3 = (bf16[4,16,125]{2,1,0:T(8,128)(2,1)S(1)}, bf16[4,16,125]{2,1,0:T(8,128)(2,1)S(1)}, u32[]{:S(2)}, u32[]{:S(2)}) collective-permute-start(bf16[4,16,125]{2,1,0:T(8,128)(2,1)S(1)} %gather_fusion.3), channel_id=1, source_target_pairs={{0,2},{1,3},{2,4},{3,5},{4,6},{5,7},{6,8},{7,9},{8,10},{9,11},{10,... | collective-permute-start | bytes 48008 | tf_op jit(solution)/shard_map/ppermute | solution.py:17
  39.5 259.5 %copy-start.6 = (s32[72]{0:T(128)}, s32[72]{0:T(128)S(1)}, u32[]{:S(2)}) copy-start(s32[72]{0:T(128)S(1)} %get-tuple-element.7) | copy-start | bytes 868
  39.7 243.0 %copy-start.10 = (pred[4]{0:T(512)(128)(4,1)}, pred[4]{0:T(512)(128)(4,1)S(1)}, u32[]{:S(2)}) copy-start(pred[4]{0:T(512)(128)(4,1)S(1)} %fusion.56) | copy-start | bytes 16
  40.0 245.3 %copy-start.12 = (pred[4]{0:T(512)(128)(4,1)}, pred[4]{0:T(512)(128)(4,1)S(1)}, u32[]{:S(2)}) copy-start(pred[4]{0:T(512)(128)(4,1)S(1)} %fusion.55) | copy-start | bytes 16
  40.2 252.2 %copy-start.8 = (pred[4]{0:T(512)(128)(4,1)}, pred[4]{0:T(512)(128)(4,1)S(1)}, u32[]{:S(2)}) copy-start(pred[4]{0:T(512)(128)(4,1)S(1)} %fusion.54) | copy-start | bytes 16
  40.5 256.3 %copy-start.14 = (pred[4]{0:T(512)(128)(4,1)}, pred[4]{0:T(512)(128)(4,1)S(1)}, u32[]{:S(2)}) copy-start(pred[4]{0:T(512)(128)(4,1)S(1)} %fusion.57) | copy-start | bytes 16
  41.2 137.0 %copy-start.16 = (pred[12]{0:T(512)(128)(4,1)}, pred[12]{0:T(512)(128)(4,1)S(1)}, u32[]{:S(2)}) copy-start(pred[12]{0:T(512)(128)(4,1)S(1)} %iota_compare_fusion.8) | copy-start | bytes 40
  279.4 28.5 %copy-start.2 = (bf16[27,16,125]{2,1,0:T(8,128)(2,1)S(1)}, bf16[27,16,125]{2,1,0:T(8,128)(2,1)}, u32[]{:S(2)}) copy-start(bf16[27,16,125]{2,1,0:T(8,128)(2,1)} %param.12) | copy-start | bytes 324004
  282.8 24.0 %collective-permute-start.5 = (bf16[4,16,125]{2,1,0:T(8,128)(2,1)S(1)}, bf16[4,16,125]{2,1,0:T(8,128)(2,1)S(1)}, u32[]{:S(2)}, u32[]{:S(2)}) collective-permute-start(bf16[4,16,125]{2,1,0:T(8,128)(2,1)S(1)} %broadcast_select_fusion.5), channel_id=1, source_target_pairs={{0,2},{1,3},{2,4},{3,5},{4,6},{5,7},{6,8},{7,9},{8,10},{9,11},{10,... | collective-permute-start | bytes 48008 | tf_op jit(solution)/shard_map/ppermute | solution.py:17
  285.4 21.5 %collective-permute-start.6 = (bf16[4,16,125]{2,1,0:T(8,128)(2,1)S(1)}, bf16[4,16,125]{2,1,0:T(8,128)(2,1)S(1)}, u32[]{:S(2)}, u32[]{:S(2)}) collective-permute-start(bf16[4,16,125]{2,1,0:T(8,128)(2,1)S(1)} %broadcast_select_fusion.3), channel_id=1, source_target_pairs={{1,0},{2,1},{3,2},{4,3},{5,4},{6,5},{7,6},{8,7},{9,8},{10,9},{11,1... | collective-permute-start | bytes 48008 | tf_op jit(solution)/shard_map/ppermute | solution.py:17
  292.5 14.3 %collective-permute-start.7 = (bf16[4,16,125]{2,1,0:T(8,128)(2,1)S(1)}, bf16[4,16,125]{2,1,0:T(8,128)(2,1)S(1)}, u32[]{:S(2)}, u32[]{:S(2)}) collective-permute-start(bf16[4,16,125]{2,1,0:T(8,128)(2,1)S(1)} %broadcast_select_fusion.1), channel_id=1, source_target_pairs={{2,0},{3,1},{4,2},{5,3},{6,4},{7,5},{8,6},{9,7},{10,8},{11,9},{12,... | collective-permute-start | bytes 48008 | tf_op jit(solution)/shard_map/ppermute | solution.py:17
  296.8 9.3 %collective-permute-start.4 = (bf16[4,16,125]{2,1,0:T(8,128)(2,1)S(1)}, bf16[4,16,125]{2,1,0:T(8,128)(2,1)S(1)}, u32[]{:S(2)}, u32[]{:S(2)}) collective-permute-start(bf16[4,16,125]{2,1,0:T(8,128)(2,1)S(1)} %broadcast_select_fusion.7), channel_id=1, source_target_pairs={{0,1},{1,2},{2,3},{3,4},{4,5},{5,6},{6,7},{7,8},{8,9},{9,10},{10,1... | collective-permute-start | bytes 48008 | tf_op jit(solution)/shard_map/ppermute | solution.py:17
  298.9 132.1 %copy-start.4 = (s32[12]{0:T(128)}, s32[12]{0:T(128)S(1)}, u32[]{:S(2)}) copy-start(s32[12]{0:T(128)S(1)} %add_bitcast_fusion) | copy-start | bytes 148
  309.5 18.2 %collective-permute-start.8 = (bf16[4,16,125]{2,1,0:T(8,128)(2,1)S(1)}, bf16[4,16,125]{2,1,0:T(8,128)(2,1)S(1)}, u32[]{:S(2)}, u32[]{:S(2)}) collective-permute-start(bf16[4,16,125]{2,1,0:T(8,128)(2,1)S(1)} %gather_fusion.11), channel_id=1, source_target_pairs={{1,0},{2,1},{3,2},{4,3},{5,4},{6,5},{7,6},{8,7},{9,8},{10,9},{11,1... | collective-permute-start | bytes 48008 | tf_op jit(solution)/shard_map/ppermute | solution.py:17
  315.7 13.5 %collective-permute-start.11 = (bf16[4,16,125]{2,1,0:T(8,128)(2,1)S(1)}, bf16[4,16,125]{2,1,0:T(8,128)(2,1)S(1)}, u32[]{:S(2)}, u32[]{:S(2)}) collective-permute-start(bf16[4,16,125]{2,1,0:T(8,128)(2,1)S(1)} %gather_fusion.14), channel_id=1, source_target_pairs={{0,2},{1,3},{2,4},{3,5},{4,6},{5,7},{6,8},{7,9},{8,10},{9,11},{10,... | collective-permute-start | bytes 48008 | tf_op jit(solution)/shard_map/ppermute | solution.py:17
  317.7 11.5 %collective-permute-start.10 = (bf16[4,16,125]{2,1,0:T(8,128)(2,1)S(1)}, bf16[4,16,125]{2,1,0:T(8,128)(2,1)S(1)}, u32[]{:S(2)}, u32[]{:S(2)}) collective-permute-start(bf16[4,16,125]{2,1,0:T(8,128)(2,1)S(1)} %gather_fusion.13), channel_id=1, source_target_pairs={{0,1},{1,2},{2,3},{3,4},{4,5},{5,6},{6,7},{7,8},{8,9},{9,10},{10,1... | collective-permute-start | bytes 48008 | tf_op jit(solution)/shard_map/ppermute | solution.py:17
  319.6 9.6 %collective-permute-start.9 = (bf16[4,16,125]{2,1,0:T(8,128)(2,1)S(1)}, bf16[4,16,125]{2,1,0:T(8,128)(2,1)S(1)}, u32[]{:S(2)}, u32[]{:S(2)}) collective-permute-start(bf16[4,16,125]{2,1,0:T(8,128)(2,1)S(1)} %gather_fusion.12), channel_id=1, source_target_pairs={{2,0},{3,1},{4,2},{5,3},{6,4},{7,5},{8,6},{9,7},{10,8},{11,9},{12,... | collective-permute-start | bytes 48008 | tf_op jit(solution)/shard_map/ppermute | solution.py:17
  433.7 6.5 %copy-start.17 = (pred[12]{0:T(512)(128)(4,1)S(1)}, pred[12]{0:T(512)(128)(4,1)}, u32[]{:S(2)}) copy-start(pred[12]{0:T(512)(128)(4,1)} %copy-done.16) | copy-start | bytes 40
  442.1 102.9 %copy-start.11 = (pred[4]{0:T(512)(128)(4,1)S(1)}, pred[4]{0:T(512)(128)(4,1)}, u32[]{:S(2)}) copy-start(pred[4]{0:T(512)(128)(4,1)} %copy-done.10) | copy-start | bytes 16
  442.1 104.9 %copy-start.13 = (pred[4]{0:T(512)(128)(4,1)S(1)}, pred[4]{0:T(512)(128)(4,1)}, u32[]{:S(2)}) copy-start(pred[4]{0:T(512)(128)(4,1)} %copy-done.12) | copy-start | bytes 16
  442.1 112.0 %copy-start.15 = (pred[4]{0:T(512)(128)(4,1)S(1)}, pred[4]{0:T(512)(128)(4,1)}, u32[]{:S(2)}) copy-start(pred[4]{0:T(512)(128)(4,1)} %copy-done.14) | copy-start | bytes 16
  442.2 114.0 %copy-start.9 = (pred[4]{0:T(512)(128)(4,1)S(1)}, pred[4]{0:T(512)(128)(4,1)}, u32[]{:S(2)}) copy-start(pred[4]{0:T(512)(128)(4,1)} %copy-done.8) | copy-start | bytes 16
  442.2 117.9 %copy-start.7 = (s32[72]{0:T(128)S(1)}, s32[72]{0:T(128)}, u32[]{:S(2)}) copy-start(s32[72]{0:T(128)} %copy-done.6) | copy-start | bytes 868
  540.1 24.5 %copy-start.5 = (s32[12]{0:T(128)S(1)}, s32[12]{0:T(128)}, u32[]{:S(2)}) copy-start(s32[12]{0:T(128)} %copy-done.4) | copy-start | bytes 148
  540.1 25.6 %copy-start.1 = (f32[27,16,125]{2,1,0:T(8,128)S(1)}, f32[27,16,125]{2,1,0:T(8,128)}, u32[]{:S(2)}) copy-start(f32[27,16,125]{2,1,0:T(8,128)} %get-tuple-element.85) | copy-start | bytes 648004
  540.1 25.6 %copy-start.3 = (bf16[27,16,125]{2,1,0:T(8,128)(2,1)S(1)}, bf16[27,16,125]{2,1,0:T(8,128)(2,1)}, u32[]{:S(2)}) copy-start(bf16[27,16,125]{2,1,0:T(8,128)(2,1)} %param.12) | copy-start | bytes 324004
  545.1 19.4 %collective-permute-start.13 = (bf16[4,16,125]{2,1,0:T(8,128)(2,1)S(1)}, bf16[4,16,125]{2,1,0:T(8,128)(2,1)S(1)}, u32[]{:S(2)}, u32[]{:S(2)}) collective-permute-start(bf16[4,16,125]{2,1,0:T(8,128)(2,1)S(1)} %broadcast_select_fusion.4), channel_id=1, source_target_pairs={{0,2},{1,3},{2,4},{3,5},{4,6},{5,7},{6,8},{7,9},{8,10},{9,11},{10,... | collective-permute-start | bytes 48008 | tf_op jit(solution)/shard_map/ppermute | solution.py:17
  547.1 17.4 %collective-permute-start.14 = (bf16[4,16,125]{2,1,0:T(8,128)(2,1)S(1)}, bf16[4,16,125]{2,1,0:T(8,128)(2,1)S(1)}, u32[]{:S(2)}, u32[]{:S(2)}) collective-permute-start(bf16[4,16,125]{2,1,0:T(8,128)(2,1)S(1)} %broadcast_select_fusion.2), channel_id=1, source_target_pairs={{1,0},{2,1},{3,2},{4,3},{5,4},{6,5},{7,6},{8,7},{9,8},{10,9},{11,1... | collective-permute-start | bytes 48008 | tf_op jit(solution)/shard_map/ppermute | solution.py:17
  554.2 9.6 %collective-permute-start.12 = (bf16[4,16,125]{2,1,0:T(8,128)(2,1)S(1)}, bf16[4,16,125]{2,1,0:T(8,128)(2,1)S(1)}, u32[]{:S(2)}, u32[]{:S(2)}) collective-permute-start(bf16[4,16,125]{2,1,0:T(8,128)(2,1)S(1)} %broadcast_select_fusion.6), channel_id=1, source_target_pairs={{0,1},{1,2},{2,3},{3,4},{4,5},{5,6},{6,7},{7,8},{8,9},{9,10},{10,1... | collective-permute-start | bytes 48008 | tf_op jit(solution)/shard_map/ppermute | solution.py:17
  556.2 8.3 %collective-permute-start.15 = (bf16[4,16,125]{2,1,0:T(8,128)(2,1)S(1)}, bf16[4,16,125]{2,1,0:T(8,128)(2,1)S(1)}, u32[]{:S(2)}, u32[]{:S(2)}) collective-permute-start(bf16[4,16,125]{2,1,0:T(8,128)(2,1)S(1)} %broadcast_select_fusion), channel_id=1, source_target_pairs={{2,0},{3,1},{4,2},{5,3},{6,4},{7,5},{8,6},{9,7},{10,8},{11,9},{12,... | collective-permute-start | bytes 48008 | tf_op jit(solution)/shard_map/ppermute | solution.py:17
where the time goes:
time: 572 us; the launch traced here: 567 us
  local copies, waits for them, and re-layouts  459 us (80%)
  starting transfers between devices  61.1 us (11%)
  other arithmetic  25.9 us (5%)
  matrix products  15.1 us (3%)
    gather x7, local copies, waits for them, and re-layouts, per_device(): jnp.take_along_axis(elem_terms.reshape(incidences, functionals, trace_len...  201 us
    gather x7, local copies, waits for them, and re-layouts, per_device(): jnp.take_along_axis(gathered, to_element[:, None, :], axis=2)  201 us
    ppermute x16, starting transfers between devices, passed_along(): return lax.ppermute(block, axis, route)  61.1 us
    reshape x1, local copies, waits for them, and re-layouts, element_terms(): blocks = matrices.reshape(matrices.shape[0], 6, trace_len, 6, trace_len)  17.1 us
    dot_general x2, matrix products, element_terms(): jnp.einsum('akni,akilj->alnj', elem_frame, blocks, preferred_element_type...  13 us
  transfers between devices with their start and end apart: 16, of which 2 were waited for; matrix products, arithmetic and copies ran while one was open for 10% of the time, Pallas kernels for 0%

commit v1 on v0

v1 whole, which is shorter than its diff:
```python
import functools

import jax
import jax.numpy as jnp
from jax import lax
from jax.experimental import pallas as pl
from jax.experimental.pallas import tpu as pltpu
from jax.sharding import PartitionSpec as P

EDGE = 5
TRACE = 125
SLOT = 4
LIVE = 9
ZERO_ROW = 116
ROUTES = (0, 1, 3, 4)
MESH = pl.DeviceIdType.MESH


def lanes_of(values, index):
    return jnp.take_along_axis(values, index, axis=1, mode="promise_in_bounds")


def code_tables():
    shape = (48, 128)
    row = lax.broadcasted_iota(jnp.int32, shape, 0)
    lane = lax.broadcasted_iota(jnp.int32, shape, 1)
    side, code = row >> 3, row & 7

    def split(i):
        comp = (i * 1311) >> 15
        rest = i - comp * 25
        first = (rest * 205) >> 10
        return comp, first, rest - first * 5

    swap, flip_p, flip_q = (code & 4) > 0, (code & 1) > 0, (code & 2) > 0
    low = lane + 3 * side
    high = lane - (128 - 3 * side)
    node = jnp.where(low < TRACE, low, jnp.where(high >= 0, high, 0))
    comp, p, q = split(node)
    p, q = jnp.where(swap, q, p), jnp.where(swap, p, q)
    p = jnp.where(flip_p, EDGE - 1 - p, p)
    q = jnp.where(flip_q, EDGE - 1 - q, q)
    forward = comp * 25 + p * 5 + q
    comp, p, q = split(jnp.minimum(lane, TRACE - 1))
    p = jnp.where(flip_p, EDGE - 1 - p, p)
    q = jnp.where(flip_q, EDGE - 1 - q, q)
    p, q = jnp.where(swap, q, p), jnp.where(swap, p, q)
    backward = (comp * 25 + p * 5 + q + TRACE * side) & 127
    return forward, backward


def index_tables(me, devices, faces, codes, shift, count_of):
    shape = (8, 128)
    row = lax.broadcasted_iota(jnp.int32, shape, 0)
    lane = lax.broadcasted_iota(jnp.int32, shape, 1)
    packed = faces * 8 + codes
    packed = jnp.concatenate([packed, jnp.zeros((2, 256), jnp.int32)], axis=0)
    packed = pltpu.roll(packed, shift, 1)[:, :128]
    take = jnp.minimum(12 * row + (lane & 15), 127)
    flat = jnp.zeros(shape, jnp.int32)
    for k in range(6):
        source = jnp.broadcast_to(packed[k : k + 1, :], shape)
        flat = jnp.where((lane >> 4) == k, lanes_of(source, take), flat)
    face = flat >> 3
    owner = (face * 9710) >> 18
    local = face - owner * 27
    device = row + (me - 2)
    count = jnp.zeros(shape, jnp.int32)
    for r in range(5):
        count = jnp.where(row == r, count_of[r], count)
    live = (
        ((lane & 15) < count)
        & (lane < 96)
        & (row < 5)
        & (device >= 0)
        & (device < devices)
    )
    key = jnp.where(live, owner, -9)
    mine_key = jnp.broadcast_to(key[2:3, :], shape)
    mine_local = jnp.broadcast_to(local[2:3, :], shape)
    mine_code = jnp.broadcast_to(flat[2:3, :] & 7, shape)
    sends = (mine_key == device) & (row < 5)
    takes = (key == me) & (row != 2)
    both = jnp.concatenate([sends.astype(jnp.int32), takes.astype(jnp.int32)], axis=0)
    lane16 = lax.broadcasted_iota(jnp.int32, (16, 128), 1)
    rank = both
    for step in (1, 2, 4, 8, 16, 32, 64):
        rank = rank + jnp.where(lane16 >= step, pltpu.roll(rank, step, 1), 0)
    rank = rank - both
    send_rank, take_rank = rank[:8], rank[8:]
    place = jnp.where(row == 2, mine_local, 27 + SLOT * row + send_rank)
    place = jnp.sum(jnp.where(sends, place, 0), axis=0, keepdims=True)
    place = jnp.broadcast_to(place, shape)
    head = jnp.where(row == 0, place, (lane >> 4) * 8 + mine_code)
    values = jnp.concatenate([lane, local], axis=0)
    slot_of = jnp.where(both > 0, rank, -1)
    picks = jnp.zeros((16, 128), jnp.int32)
    for s in range(SLOT):
        found = jnp.sum(jnp.where(slot_of == s, values, 0), axis=1, keepdims=True)
        picks = jnp.where(lane16 == s, found, picks)
    first = jnp.concatenate([head, picks], axis=0)

    home = jnp.where(mine_key == me, local, -1)
    match = jnp.where(row == 2, home, jnp.where(takes, local, -1))
    source = jnp.where(row == 2, lane, 96 + SLOT * row + take_rank)
    tall = (32, 128)
    own = lax.broadcasted_iota(jnp.int32, tall, 0)
    lane32 = lax.broadcasted_iota(jnp.int32, tall, 1)
    most = jnp.full(tall, -1, jnp.int32)
    least = jnp.full(tall, 999, jnp.int32)
    for r in range(5):
        same = jnp.broadcast_to(match[r : r + 1, :], tall) == own
        value = jnp.broadcast_to(source[r : r + 1, :], tall)
        most = jnp.maximum(most, jnp.where(same, value, -1))
        least = jnp.minimum(least, jnp.where(same, value, 999))
    most = jnp.max(most, axis=1, keepdims=True)
    least = jnp.min(least, axis=1, keepdims=True)
    one = jnp.where(most < 0, ZERO_ROW, most)
    two = jnp.where(least >= most, ZERO_ROW, least)
    second = jnp.where(lane32 == 0, one, jnp.where(lane32 == 1, two, 0))
    return first, second


def kernel(
    devices,
    mats_hbm, blocks_hbm, rhs_hbm, faces_hbm, codes_hbm, counts_hbm,
    out_ref,
    mats, blocks, rhs, faces, codes, counts,
    first_v, second_v, first_s, second_s, forward, backward,
    table, solved, frames, terms, send_one, recv_one, send_two, recv_two,
    mat_sem, load_sem, send_sem, recv_sem,
):
    me = lax.axis_index("elem")
    start = 12 * me - 24
    base = pl.multiple_of(jnp.clip((start // 128) * 128, 0, faces_hbm.shape[1] - 256), 128)
    shift = (256 - (start - base)) % 256
    window = pl.ds(base, 256)
    loads = [
        pltpu.make_async_copy(faces_hbm.at[:, window], faces, load_sem.at[0]),
        pltpu.make_async_copy(codes_hbm.at[:, window], codes, load_sem.at[1]),
        pltpu.make_async_copy(counts_hbm, counts, load_sem.at[2]),
        pltpu.make_async_copy(rhs_hbm, rhs, load_sem.at[3]),
        pltpu.make_async_copy(blocks_hbm, blocks, load_sem.at[4]),
    ]
    for load in loads:
        load.start()
    barrier = pltpu.get_barrier_semaphore()
    peers = [lax.rem(me + (r - 2 + devices), devices) for r in range(5)]
    for r in ROUTES:
        pl.semaphore_signal(barrier, inc=1, device_id=(peers[r],), device_id_type=MESH)
    mat_loads = [
        pltpu.make_async_copy(mats_hbm.at[e], mats.at[e], mat_sem.at[e]) for e in range(LIVE)
    ]
    for load in mat_loads:
        load.start()

    table[...] = jnp.zeros_like(table)
    terms[...] = jnp.zeros_like(terms)
    forward[...], backward[...] = code_tables()

    for load in loads[:3]:
        load.wait()
    count_of = [counts[0, jnp.clip(me - 2 + r, 0, devices - 1)] for r in range(5)]
    first_v[...], second_v[...] = index_tables(
        me, devices, faces[...], codes[...], shift, count_of
    )
    tables = [
        pltpu.make_async_copy(first_v, first_s, load_sem.at[5]),
        pltpu.make_async_copy(second_v, second_s, load_sem.at[6]),
    ]
    for copy in tables:
        copy.start()

    loads[3].wait()
    loads[4].wait()
    for f in range(27):
        value = jnp.dot(rhs[f], blocks[f], preferred_element_type=jnp.float32)
        solved[f] = value
        table[f, :, :TRACE] = value.astype(jnp.bfloat16)

    for copy in tables:
        copy.wait()

    def route(send, recv, leg, r, slot):
        return pltpu.make_async_remote_copy(
            src_ref=send.at[pl.ds(SLOT * r, SLOT)],
            dst_ref=recv.at[pl.ds(SLOT * slot, SLOT)],
            send_sem=send_sem.at[leg, r],
            recv_sem=recv_sem.at[leg, slot],
            device_id=(peers[r],),
            device_id_type=MESH,
        )

    def exchange(send, recv, leg):
        for r in ROUTES:
            route(send, recv, leg, r, 4 - r).start()

    def settle(send, recv, leg):
        for r in ROUTES:
            route(send, recv, leg, r, r).wait_recv()

    for r in ROUTES:
        for s in range(SLOT):
            send_one[SLOT * r + s] = table[first_s[16 + r, s]]
    pl.semaphore_wait(barrier, 4)
    exchange(send_one, recv_one, 0)
    settle(send_one, recv_one, 0)
    for r in ROUTES:
        table[27 + SLOT * r : 27 + SLOT * (r + 1)] = recv_one[SLOT * r : SLOT * (r + 1)]

    lane = lax.broadcasted_iota(jnp.int32, (16, 128), 1)

    def gather_frame(e):
        pieces = []
        for k in range(6):
            value = table[first_s[0, k * 16 + e]].astype(jnp.float32)
            index = forward[pl.ds(first_s[1, k * 16 + e], 1), :]
            pieces.append(lanes_of(value, jnp.broadcast_to(index, (16, 128))))
        pieces.append(jnp.zeros((16, 128), jnp.float32))
        for c in range(6):
            column = jnp.where(lane < TRACE - 3 * c, pieces[c], pieces[c + 1])
            frames[e, :, 128 * c : 128 * (c + 1)] = column.astype(jnp.bfloat16)

    for e in range(LIVE):
        gather_frame(e)

    def apply(e, carry):
        pltpu.make_async_copy(mats_hbm.at[e], mats.at[e], mat_sem.at[e]).wait()
        value = jnp.dot(frames[e, :, :750], mats[e], preferred_element_type=jnp.float32)
        value = value.astype(jnp.bfloat16).astype(jnp.float32)
        value = jnp.concatenate([value, jnp.zeros((16, 18), jnp.float32)], axis=1)
        columns = [value[:, 128 * c : 128 * (c + 1)] for c in range(6)]
        for k in range(6):
            held = columns[k]
            if k:
                held = jnp.where(lane < TRACE - 3 * k, columns[k], columns[k - 1])
            index = backward[pl.ds(first_s[1, k * 16 + e], 1), :]
            moved = lanes_of(held, jnp.broadcast_to(index, (16, 128)))
            terms[k * 16 + e] = moved.astype(jnp.bfloat16)
        return carry

    lax.fori_loop(0, LIVE, apply, 0)

    for r in ROUTES:
        for s in range(SLOT):
            send_two[SLOT * r + s] = terms[first_s[8 + r, s]]
    exchange(send_two, recv_two, 1)
    settle(send_two, recv_two, 1)
    for r in ROUTES:
        terms[96 + SLOT * r : 96 + SLOT * (r + 1)] = recv_two[SLOT * r : SLOT * (r + 1)]

    for f in range(27):
        summed = terms[second_s[f, 0]].astype(jnp.float32) + terms[second_s[f, 1]].astype(
            jnp.float32
        )
        residual = (rhs[f].astype(jnp.float32) - summed[:, :TRACE]).astype(jnp.bfloat16)
        out_ref[f] = solved[f] + jnp.dot(
            residual, blocks[f], preferred_element_type=jnp.float32
        )
    for r in ROUTES:
        route(send_one, recv_one, 0, r, 4 - r).wait_send()
        route(send_two, recv_two, 1, r, 4 - r).wait_send()


def solution(mesh):
    devices = mesh.shape["elem"]

    def per_device(elem_mats, face_blocks, rhs, elem_faces, orient, counts):
        faces, functionals, trace = rhs.shape
        return pl.pallas_call(
            functools.partial(kernel, devices),
            name="sweeps",
            out_shape=jax.ShapeDtypeStruct(rhs.shape, jnp.float32),
            in_specs=[pl.BlockSpec(memory_space=pl.ANY)] * 6,
            out_specs=pl.BlockSpec(memory_space=pltpu.VMEM),
            scratch_shapes=[
                pltpu.VMEM((LIVE, 750, 750), jnp.bfloat16),
                pltpu.VMEM((faces, trace, trace), jnp.bfloat16),
                pltpu.VMEM((faces, functionals, trace), jnp.bfloat16),
                pltpu.VMEM((6, 256), jnp.int32),
                pltpu.VMEM((6, 256), jnp.int32),
                pltpu.SMEM((1, devices), jnp.int32),
                pltpu.VMEM((24, 128), jnp.int32),
                pltpu.VMEM((32, 128), jnp.int32),
                pltpu.SMEM((24, 128), jnp.int32),
                pltpu.SMEM((32, 128), jnp.int32),
                pltpu.VMEM((48, 128), jnp.int32),
                pltpu.VMEM((48, 128), jnp.int32),
                pltpu.VMEM((47, 16, 128), jnp.bfloat16),
                pltpu.VMEM((faces, functionals, trace), jnp.float32),
                pltpu.VMEM((LIVE, 16, 768), jnp.bfloat16),
                pltpu.VMEM((117, 16, 128), jnp.bfloat16),
                pltpu.VMEM((20, 16, 128), jnp.bfloat16),
                pltpu.VMEM((20, 16, 128), jnp.bfloat16),
                pltpu.VMEM((20, 16, 128), jnp.bfloat16),
                pltpu.VMEM((20, 16, 128), jnp.bfloat16),
                pltpu.SemaphoreType.DMA((LIVE,)),
                pltpu.SemaphoreType.DMA((7,)),
                pltpu.SemaphoreType.DMA((2, 5)),
                pltpu.SemaphoreType.DMA((2, 5)),
            ],
            compiler_params=pltpu.CompilerParams(collective_id=0, has_side_effects=True),
        )(elem_mats, face_blocks, rhs, elem_faces.T, orient.T, counts.reshape(1, -1))

    in_specs = (P("elem", None, None), P("elem", None, None), P("elem", None, None), P(), P(), P())
    return jax.shard_map(
        per_device, mesh=mesh, in_specs=in_specs, out_specs=P("elem", None, None), check_vma=False
    )
```

time: 572 us -> 26.7 us (0.05)
  the two profiles are of different devices: /device:TPU:6 before, /device:TPU:1 now
where the time goes in v1:
time: 26.7 us; the launch traced here: 26.6 us
  Pallas kernels  24.9 us (93%)
  local copies, waits for them, and re-layouts  1.64 us (6%)
    pallas_call x1, Pallas kernels, per_device(): pl.pallas_call(functools.partial(kernel, devices), name='sweeps', out_sha...  24.9 us
    unnamed x1, local copies, waits for them, and re-layouts  1.64 us

profile of v1, /device:TPU:1, one launch (start us, length us, event | category | flops | bytes accessed | tf_op | source)
XLA Modules:
  0.0 26.6 jit_solution(12417482672539328029)
XLA Ops:
  0.0 24.9 %sweeps.1 = f32[27,16,125]{2,1,0:T(8,128)} custom-call(bf16[12,750,750]{2,1,0:T(8,128)(2,1)} %mats_hbm.1, bf16[27,125,125]{2,1,0:T(8,128)(2,1)} %blocks_hbm.1, bf16[27,16,125]{2,1,0:T(8,128)(2,1)} %rhs_hbm.1, s32[6,1536]{1,0:T(8,128)} %bitcast.3, s32[6,1536]{1,0:T(8,128)} %bitcast.4, s32[1,128]{1,0:T(1,128)} %bitcast.5), custom_call_target="tpu_custom_call" | custom-call | tf_op jit(solution)/shard_map/sweeps/pallas_call | solution.py:270
  24.9 1.6 %copy.8 = f32[27,16,125]{2,1,0:T(8,128)} copy(f32[27,16,125]{2,1,0:T(8,128)} %sweeps.1) | data formatting | bytes 432000

commit v2 on v1

--- a/solution.py
+++ b/solution.py
@@ -145,9 +145,14 @@
     for load in loads:
         load.start()
     barrier = pltpu.get_barrier_semaphore()
-    peers = [lax.rem(me + (r - 2 + devices), devices) for r in range(5)]
-    for r in ROUTES:
-        pl.semaphore_signal(barrier, inc=1, device_id=(peers[r],), device_id_type=MESH)
+    peers = [me + (r - 2) for r in range(5)]
+    exists = [(me >= 2 - r) if r < 2 else (me < devices + 2 - r) for r in range(5)]
+    for r in ROUTES:
+
+        @pl.when(exists[r])
+        def _(r=r):
+            pl.semaphore_signal(barrier, inc=1, device_id=(peers[r],), device_id_type=MESH)
+
     mat_loads = [
         pltpu.make_async_copy(mats_hbm.at[e], mats.at[e], mat_sem.at[e]) for e in range(LIVE)
     ]
@@ -193,16 +198,23 @@
 
     def exchange(send, recv, leg):
         for r in ROUTES:
-            route(send, recv, leg, r, 4 - r).start()
+
+            @pl.when(exists[r])
+            def _(r=r):
+                route(send, recv, leg, r, 4 - r).start()
 
     def settle(send, recv, leg):
         for r in ROUTES:
-            route(send, recv, leg, r, r).wait_recv()
+
+            @pl.when(exists[r])
+            def _(r=r):
+                route(send, recv, leg, r, r).wait_recv()
 
     for r in ROUTES:
         for s in range(SLOT):
             send_one[SLOT * r + s] = table[first_s[16 + r, s]]
-    pl.semaphore_wait(barrier, 4)
+    heard = 4 - jnp.maximum(2 - me, 0) - jnp.maximum(me - (devices - 3), 0)
+    pl.semaphore_wait(barrier, heard)
     exchange(send_one, recv_one, 0)
     settle(send_one, recv_one, 0)
     for r in ROUTES:
@@ -258,8 +270,11 @@
             residual, blocks[f], preferred_element_type=jnp.float32
         )
     for r in ROUTES:
-        route(send_one, recv_one, 0, r, 4 - r).wait_send()
-        route(send_two, recv_two, 1, r, 4 - r).wait_send()
+
+        @pl.when(exists[r])
+        def _(r=r):
+            route(send_one, recv_one, 0, r, 4 - r).wait_send()
+            route(send_two, recv_two, 1, r, 4 - r).wait_send()
 
 
 def solution(mesh):

time: 26.7 us -> 23 us (0.86)
  the two profiles are of different devices: /device:TPU:1 before, /device:TPU:6 now
where the time goes in v2:
time: 23 us; the launch traced here: 22.9 us
  Pallas kernels  21.3 us (93%)
  local copies, waits for them, and re-layouts  1.64 us (7%)
    pallas_call x1, Pallas kernels, per_device(): pl.pallas_call(functools.partial(kernel, devices), name='sweeps', out_sha...  21.3 us
    unnamed x1, local copies, waits for them, and re-layouts  1.64 us

profile of v2, /device:TPU:6, one launch (start us, length us, event | category | flops | bytes accessed | tf_op | source)
XLA Modules:
  0.0 22.9 jit_solution(4339896542914472518)
XLA Ops:
  0.0 21.3 %sweeps.1 = f32[27,16,125]{2,1,0:T(8,128)} custom-call(bf16[12,750,750]{2,1,0:T(8,128)(2,1)} %mats_hbm.1, bf16[27,125,125]{2,1,0:T(8,128)(2,1)} %blocks_hbm.1, bf16[27,16,125]{2,1,0:T(8,128)(2,1)} %rhs_hbm.1, s32[6,1536]{1,0:T(8,128)} %bitcast.3, s32[6,1536]{1,0:T(8,128)} %bitcast.4, s32[1,128]{1,0:T(1,128)} %bitcast.5), custom_call_target="tpu_custom_call" | custom-call | tf_op jit(solution)/shard_map/sweeps/pallas_call | solution.py:285
  21.3 1.6 %copy.8 = f32[27,16,125]{2,1,0:T(8,128)} copy(f32[27,16,125]{2,1,0:T(8,128)} %sweeps.1) | data formatting | bytes 432000

commit v3 on v2

--- a/solution.py
+++ b/solution.py
@@ -13,6 +13,7 @@
 LIVE = 9
 ZERO_ROW = 116
 ROUTES = (0, 1, 3, 4)
+PLANE = 32
 MESH = pl.DeviceIdType.MESH
 
 
@@ -128,7 +129,7 @@
     mats, blocks, rhs, faces, codes, counts,
     first_v, second_v, first_s, second_s, forward, backward,
     table, solved, frames, terms, send_one, recv_one, send_two, recv_two,
-    mat_sem, load_sem, send_sem, recv_sem,
+    relay, mat_sem, load_sem, send_sem, recv_sem, relay_sem,
 ):
     me = lax.axis_index("elem")
     start = 12 * me - 24
@@ -147,12 +148,30 @@
     barrier = pltpu.get_barrier_semaphore()
     peers = [me + (r - 2) for r in range(5)]
     exists = [(me >= 2 - r) if r < 2 else (me < devices + 2 - r) for r in range(5)]
-    for r in ROUTES:
-
-        @pl.when(exists[r])
-        def _(r=r):
-            pl.semaphore_signal(barrier, inc=1, device_id=(peers[r],), device_id_type=MESH)
-
+    place = lax.rem(me, PLANE)
+    late = (place >= PLANE - 2) & (me < devices - PLANE)
+    late_one = (place == PLANE - 1) & (me < devices - PLANE)
+    early = (place < 2) & (me >= PLANE)
+    early_zero = (place == 0) & (me >= PLANE)
+    relays = (place >= PLANE - 8) & (place < PLANE - 6) & (me < devices - PLANE)
+    relays_zero = (place == PLANE - 8) & (me < devices - PLANE)
+    greets = list(exists)
+    greets[3] = exists[3] & jnp.logical_not(late_one)
+    greets[4] = exists[4] & jnp.logical_not(late)
+    direct = list(exists)
+    direct[0] = exists[0] & jnp.logical_not(early)
+    direct[1] = exists[1] & jnp.logical_not(early_zero)
+    signals = [(greets[r], peers[r]) for r in ROUTES]
+    signals += [(late, me - 6), (late_one, me - 7), (relays, me + 8)]
+    for wanted, peer in signals:
+
+        @pl.when(wanted)
+        def _(peer=peer):
+            pl.semaphore_signal(barrier, inc=1, device_id=(peer,), device_id_type=MESH)
+
+    heard = 4 - jnp.maximum(2 - me, 0) - jnp.maximum(me - (devices - 3), 0)
+    heard = heard - early_zero.astype(jnp.int32)
+    heard = heard + relays.astype(jnp.int32) + relays_zero.astype(jnp.int32)
     mat_loads = [
         pltpu.make_async_copy(mats_hbm.at[e], mats.at[e], mat_sem.at[e]) for e in range(LIVE)
     ]
@@ -196,12 +215,39 @@
             device_id_type=MESH,
         )
 
-    def exchange(send, recv, leg):
+    def exchange(send, recv, leg, sends):
         for r in ROUTES:
 
-            @pl.when(exists[r])
+            @pl.when(sends[r])
             def _(r=r):
                 route(send, recv, leg, r, 4 - r).start()
+
+    def to_relay(r):
+        return pltpu.make_async_remote_copy(
+            src_ref=send_one.at[pl.ds(SLOT * r, SLOT)],
+            dst_ref=relay.at[pl.ds(SLOT * r, SLOT)],
+            send_sem=relay_sem.at[0, r],
+            recv_sem=relay_sem.at[1, r],
+            device_id=(me - 8,),
+            device_id_type=MESH,
+        )
+
+    def onward(r):
+        return pltpu.make_async_remote_copy(
+            src_ref=relay.at[pl.ds(SLOT * r, SLOT)],
+            dst_ref=recv_one.at[pl.ds(SLOT * (4 - r), SLOT)],
+            send_sem=relay_sem.at[2, r],
+            recv_sem=recv_sem.at[0, 4 - r],
+            device_id=(me + 6 + r,),
+            device_id_type=MESH,
+        )
+
+    def when_each(conditions, act):
+        for r, wanted in enumerate(conditions):
+
+            @pl.when(wanted)
+            def _(r=r):
+                act(r)
 
     def settle(send, recv, leg):
         for r in ROUTES:
@@ -213,9 +259,15 @@
     for r in ROUTES:
         for s in range(SLOT):
             send_one[SLOT * r + s] = table[first_s[16 + r, s]]
-    heard = 4 - jnp.maximum(2 - me, 0) - jnp.maximum(me - (devices - 3), 0)
     pl.semaphore_wait(barrier, heard)
-    exchange(send_one, recv_one, 0)
+    when_each((early, early_zero), lambda r: to_relay(r).start())
+    exchange(send_one, recv_one, 0, direct)
+
+    def forward_on(r):
+        to_relay(r).wait_recv()
+        onward(r).start()
+
+    when_each((relays, relays_zero), forward_on)
     settle(send_one, recv_one, 0)
     for r in ROUTES:
         table[27 + SLOT * r : 27 + SLOT * (r + 1)] = recv_one[SLOT * r : SLOT * (r + 1)]
@@ -256,7 +308,7 @@
     for r in ROUTES:
         for s in range(SLOT):
             send_two[SLOT * r + s] = terms[first_s[8 + r, s]]
-    exchange(send_two, recv_two, 1)
+    exchange(send_two, recv_two, 1, exists)
     settle(send_two, recv_two, 1)
     for r in ROUTES:
         terms[96 + SLOT * r : 96 + SLOT * (r + 1)] = recv_two[SLOT * r : SLOT * (r + 1)]
@@ -269,11 +321,16 @@
         out_ref[f] = solved[f] + jnp.dot(
             residual, blocks[f], preferred_element_type=jnp.float32
         )
-    for r in ROUTES:
+    when_each((early, early_zero), lambda r: to_relay(r).wait_send())
+    when_each((relays, relays_zero), lambda r: onward(r).wait_send())
+    for r in ROUTES:
+
+        @pl.when(direct[r])
+        def _(r=r):
+            route(send_one, recv_one, 0, r, 4 - r).wait_send()
 
         @pl.when(exists[r])
         def _(r=r):
-            route(send_one, recv_one, 0, r, 4 - r).wait_send()
             route(send_two, recv_two, 1, r, 4 - r).wait_send()
 
 
@@ -285,7 +342,7 @@
         return pl.pallas_call(
             functools.partial(kernel, devices),
             name="sweeps",
-            out_shape=jax.ShapeDtypeStruct(rhs.shape, jnp.float32),
+            out_shape=pltpu.VMEM(rhs.shape, jnp.float32),
             in_specs=[pl.BlockSpec(memory_space=pl.ANY)] * 6,
             out_specs=pl.BlockSpec(memory_space=pltpu.VMEM),
             scratch_shapes=[
@@ -309,10 +366,12 @@
                 pltpu.VMEM((20, 16, 128), jnp.bfloat16),
                 pltpu.VMEM((20, 16, 128), jnp.bfloat16),
                 pltpu.VMEM((20, 16, 128), jnp.bfloat16),
+                pltpu.VMEM((8, 16, 128), jnp.bfloat16),
                 pltpu.SemaphoreType.DMA((LIVE,)),
                 pltpu.SemaphoreType.DMA((7,)),
                 pltpu.SemaphoreType.DMA((2, 5)),
                 pltpu.SemaphoreType.DMA((2, 5)),
+                pltpu.SemaphoreType.DMA((3, 2)),
             ],
             compiler_params=pltpu.CompilerParams(collective_id=0, has_side_effects=True),
         )(elem_mats, face_blocks, rhs, elem_faces.T, orient.T, counts.reshape(1, -1))

time: 23 us -> 20.3 us (0.88)
  Pallas kernels: 21.3 us -> 19.4 us
  local copies, waits for them, and re-layouts: 1.64 us -> 0.69 us
    pallas_call x1, Pallas kernels: 21.3 us -> 19.4 us  [per_device(): pl.pallas_call(functools.partial(kernel, devices), name='sweeps', out_sha...]
    unnamed x1, local copies, waits for them, and re-layouts: 1.64 us -> 0.69 us
where the time goes in v3:
time: 20.3 us; the launch traced here: 20.1 us
  Pallas kernels  19.4 us (96%)
  local copies, waits for them, and re-layouts  0.69 us (3%)
    pallas_call x1, Pallas kernels, per_device(): pl.pallas_call(functools.partial(kernel, devices), name='sweeps', out_sha...  19.4 us
    unnamed x1, local copies, waits for them, and re-layouts  0.69 us

profile of v3, /device:TPU:6, one launch (start us, length us, event | category | flops | bytes accessed | tf_op | source)
XLA Modules:
  0.0 20.1 jit_solution(8086770055390346689)
XLA Ops:
  0.0 19.4 %sweeps.1 = f32[27,16,125]{2,1,0:T(8,128)S(1)} custom-call(bf16[12,750,750]{2,1,0:T(8,128)(2,1)} %mats_hbm.1, bf16[27,125,125]{2,1,0:T(8,128)(2,1)} %blocks_hbm.1, bf16[27,16,125]{2,1,0:T(8,128)(2,1)} %rhs_hbm.1, s32[6,1536]{1,0:T(8,128)} %bitcast.3, s32[6,1536]{1,0:T(8,128)} %bitcast.4, s32[1,128]{1,0:T(1,128)} %bitcast.5), custom_call_target="tpu_custom_call" | custom-call | tf_op jit(solution)/shard_map/sweeps/pallas_call | solution.py:342
  19.5 0.7 %copy.8 = f32[27,16,125]{2,1,0:T(8,128)} copy(f32[27,16,125]{2,1,0:T(8,128)S(1)} %sweeps.1) | data formatting | bytes 432000

commit v4 on v3

--- a/solution.py
+++ b/solution.py
@@ -11,7 +11,10 @@
 TRACE = 125
 SLOT = 4
 LIVE = 9
-ZERO_ROW = 116
+ARRIVED = 72
+ZERO_ROW = 92
+WINDOW = 142
+REMOTE = 16
 ROUTES = (0, 1, 3, 4)
 PLANE = 32
 MESH = pl.DeviceIdType.MESH
@@ -47,7 +50,22 @@
     q = jnp.where(flip_q, EDGE - 1 - q, q)
     p, q = jnp.where(swap, q, p), jnp.where(swap, p, q)
     backward = (comp * 25 + p * 5 + q + TRACE * side) & 127
-    return forward, backward
+    skew = row_skew(side)
+    node = jnp.where(lane >= skew, lane - skew, lane + 128 - skew)
+    comp, p, q = split(jnp.where(node < TRACE, node, 0))
+    p, q = jnp.where(swap, q, p), jnp.where(swap, p, q)
+    p = jnp.where(flip_p, EDGE - 1 - p, p)
+    q = jnp.where(flip_q, EDGE - 1 - q, q)
+    skewed = comp * 25 + p * 5 + q
+    return forward, backward, skewed
+
+
+def row_start(side):
+    return jnp.where(side == 5, 608, ((TRACE * side) >> 4) << 4)
+
+
+def row_skew(side):
+    return TRACE * side - row_start(side)
 
 
 def index_tables(me, devices, faces, codes, shift, count_of):
@@ -57,11 +75,11 @@
     packed = faces * 8 + codes
     packed = jnp.concatenate([packed, jnp.zeros((2, 256), jnp.int32)], axis=0)
     packed = pltpu.roll(packed, shift, 1)[:, :128]
-    take = jnp.minimum(12 * row + (lane & 15), 127)
+    take = jnp.minimum(12 * row + (lane >> 3), 127)
     flat = jnp.zeros(shape, jnp.int32)
     for k in range(6):
         source = jnp.broadcast_to(packed[k : k + 1, :], shape)
-        flat = jnp.where((lane >> 4) == k, lanes_of(source, take), flat)
+        flat = jnp.where((lane & 7) == k, lanes_of(source, take), flat)
     face = flat >> 3
     owner = (face * 9710) >> 18
     local = face - owner * 27
@@ -70,8 +88,8 @@
     for r in range(5):
         count = jnp.where(row == r, count_of[r], count)
     live = (
-        ((lane & 15) < count)
-        & (lane < 96)
+        ((lane >> 3) < count)
+        & ((lane & 7) < 6)
         & (row < 5)
         & (device >= 0)
         & (device < devices)
@@ -82,28 +100,51 @@
     mine_code = jnp.broadcast_to(flat[2:3, :] & 7, shape)
     sends = (mine_key == device) & (row < 5)
     takes = (key == me) & (row != 2)
-    both = jnp.concatenate([sends.astype(jnp.int32), takes.astype(jnp.int32)], axis=0)
+    sent = jnp.where(sends & (row != 2), 1, 0)
+    remote = jnp.broadcast_to(jnp.sum(sent, axis=0, keepdims=True), shape)
+    upper = jnp.where(row == 5, remote, jnp.where(sends, 1, 0))
+    both = jnp.concatenate([upper, takes.astype(jnp.int32)], axis=0)
     lane16 = lax.broadcasted_iota(jnp.int32, (16, 128), 1)
     rank = both
     for step in (1, 2, 4, 8, 16, 32, 64):
         rank = rank + jnp.where(lane16 >= step, pltpu.roll(rank, step, 1), 0)
     rank = rank - both
     send_rank, take_rank = rank[:8], rank[8:]
-    place = jnp.where(row == 2, mine_local, 27 + SLOT * row + send_rank)
-    place = jnp.sum(jnp.where(sends, place, 0), axis=0, keepdims=True)
-    place = jnp.broadcast_to(place, shape)
-    head = jnp.where(row == 0, place, (lane >> 4) * 8 + mine_code)
-    values = jnp.concatenate([lane, local], axis=0)
+    place = jnp.where(mine_key == me, mine_local, 27)
+    side = lane & 7
+    code = side * 8 + mine_code
+    order = jnp.broadcast_to(send_rank[5:6, :], shape)
+    slot = jnp.sum(jnp.where(sent > 0, SLOT * row + send_rank, 0), axis=0, keepdims=True)
+    slot = jnp.broadcast_to(slot, shape)
+    inner = remote
+    for step in (1, 2, 4):
+        inner = inner + jnp.where(side >= step, pltpu.roll(inner, step, 1), 0)
+    fields = jnp.where(row == 0, slot, jnp.where(row == 1, code, lane >> 3))
+    fields = jnp.where(row == 3, row_start(side) >> 4, fields)
+    fields = jnp.where(row == 4, row_skew(side), fields)
+    fields = jnp.where(row == 5, jnp.where(inner == remote, 0, 1), fields)
+    queue = jnp.where(remote > 0, order, -1)
+    listed = jnp.zeros(shape, jnp.int32)
+    for q in range(REMOTE):
+        found = jnp.sum(jnp.where(queue == q, fields, 0), axis=1, keepdims=True)
+        listed = jnp.where(lane == q, found, listed)
+    last = jnp.where((side == 7) & (inner > 0), order + remote, 0)
+    for step in (1, 2, 4):
+        last = last + pltpu.roll(last, 128 - step, 1)
+    listed = jnp.where(row == 6, last, listed)
+    head = jnp.where(row == 0, place, code)
+    packed = code | ((lane >> 3) << 8) | (last << 16)
+    values = jnp.concatenate([packed, local], axis=0)
     slot_of = jnp.where(both > 0, rank, -1)
     picks = jnp.zeros((16, 128), jnp.int32)
     for s in range(SLOT):
         found = jnp.sum(jnp.where(slot_of == s, values, 0), axis=1, keepdims=True)
         picks = jnp.where(lane16 == s, found, picks)
-    first = jnp.concatenate([head, picks], axis=0)
+    first = jnp.concatenate([head, picks, listed], axis=0)
 
     home = jnp.where(mine_key == me, local, -1)
     match = jnp.where(row == 2, home, jnp.where(takes, local, -1))
-    source = jnp.where(row == 2, lane, 96 + SLOT * row + take_rank)
+    source = jnp.where(row == 2, lane, ARRIVED + SLOT * row + take_rank)
     tall = (32, 128)
     own = lax.broadcasted_iota(jnp.int32, tall, 0)
     lane32 = lax.broadcasted_iota(jnp.int32, tall, 1)
@@ -127,8 +168,8 @@
     mats_hbm, blocks_hbm, rhs_hbm, faces_hbm, codes_hbm, counts_hbm,
     out_ref,
     mats, blocks, rhs, faces, codes, counts,
-    first_v, second_v, first_s, second_s, forward, backward,
-    table, solved, frames, terms, send_one, recv_one, send_two, recv_two,
+    first_v, second_v, first_s, second_s, forward, backward, skewed,
+    table, solved, frames, shifted, home, sums, terms, send_one, recv_one, send_two, recv_two,
     relay, mat_sem, load_sem, send_sem, recv_sem, relay_sem,
 ):
     me = lax.axis_index("elem")
@@ -180,7 +221,8 @@
 
     table[...] = jnp.zeros_like(table)
     terms[...] = jnp.zeros_like(terms)
-    forward[...], backward[...] = code_tables()
+    sums[0] = jnp.zeros_like(sums[0])
+    forward[...], backward[...], skewed[...] = code_tables()
 
     for load in loads[:3]:
         load.wait()
@@ -267,51 +309,78 @@
         to_relay(r).wait_recv()
         onward(r).start()
 
-    when_each((relays, relays_zero), forward_on)
-    settle(send_one, recv_one, 0)
-    for r in ROUTES:
-        table[27 + SLOT * r : 27 + SLOT * (r + 1)] = recv_one[SLOT * r : SLOT * (r + 1)]
-
     lane = lax.broadcasted_iota(jnp.int32, (16, 128), 1)
 
-    def gather_frame(e):
+    def turned(value, codes_ref, code):
+        index = codes_ref[pl.ds(code, 1), :]
+        return lanes_of(value, jnp.broadcast_to(index, (16, 128)))
+
+    for e in range(LIVE):
         pieces = []
         for k in range(6):
-            value = table[first_s[0, k * 16 + e]].astype(jnp.float32)
-            index = forward[pl.ds(first_s[1, k * 16 + e], 1), :]
-            pieces.append(lanes_of(value, jnp.broadcast_to(index, (16, 128))))
+            value = table[first_s[0, 8 * e + k]].astype(jnp.float32)
+            pieces.append(turned(value, forward, first_s[1, 8 * e + k]))
         pieces.append(jnp.zeros((16, 128), jnp.float32))
         for c in range(6):
             column = jnp.where(lane < TRACE - 3 * c, pieces[c], pieces[c + 1])
             frames[e, :, 128 * c : 128 * (c + 1)] = column.astype(jnp.bfloat16)
 
-    for e in range(LIVE):
-        gather_frame(e)
+    def columns(ref, at, value):
+        for c in range(5):
+            ref[at, c + 1] = value[:, 128 * c : 128 * (c + 1)]
+        ref[at, 6, :, :110] = value[:, 640:750]
 
     def apply(e, carry):
         pltpu.make_async_copy(mats_hbm.at[e], mats.at[e], mat_sem.at[e]).wait()
         value = jnp.dot(frames[e, :, :750], mats[e], preferred_element_type=jnp.float32)
+        columns(home, e, value)
+        return carry
+
+    lax.fori_loop(0, 5, apply, 0)
+    when_each((relays, relays_zero), forward_on)
+    lax.fori_loop(5, LIVE, apply, 0)
+
+    settle(send_one, recv_one, 0)
+    total = None
+    for q in range(REMOTE):
+        slot, code, e, start_row, skew, adds = [first_s[24 + i, q] for i in range(6)]
+        value = turned(recv_one[slot].astype(jnp.float32), skewed, code)
+        node = lane - skew
+        main = jnp.where((node >= 0) & (node < TRACE), value, 0.0)
+        rest = jnp.where(lane <= skew - 4, value, 0.0)
+        shifted[q, :, :128] = main.astype(jnp.bfloat16)
+        shifted[q, :, 128:] = rest.astype(jnp.bfloat16)
+        rows = pl.ds(start_row * 16, WINDOW)
+        part = jnp.dot(
+            shifted[q, :, :WINDOW], mats[e, rows, :], preferred_element_type=jnp.float32
+        )
+        total = part if total is None else part + total * adds.astype(jnp.float32)
+        columns(sums, q + 1, total)
+
+    def term(e, k, last, code):
+        value = jnp.where(
+            lane < TRACE - 3 * k,
+            home[e, k + 1] + sums[last, k + 1],
+            home[e, k] + sums[last, k],
+        )
         value = value.astype(jnp.bfloat16).astype(jnp.float32)
-        value = jnp.concatenate([value, jnp.zeros((16, 18), jnp.float32)], axis=1)
-        columns = [value[:, 128 * c : 128 * (c + 1)] for c in range(6)]
-        for k in range(6):
-            held = columns[k]
-            if k:
-                held = jnp.where(lane < TRACE - 3 * k, columns[k], columns[k - 1])
-            index = backward[pl.ds(first_s[1, k * 16 + e], 1), :]
-            moved = lanes_of(held, jnp.broadcast_to(index, (16, 128)))
-            terms[k * 16 + e] = moved.astype(jnp.bfloat16)
-        return carry
-
-    lax.fori_loop(0, LIVE, apply, 0)
+        return turned(value, backward, code).astype(jnp.bfloat16)
 
     for r in ROUTES:
         for s in range(SLOT):
-            send_two[SLOT * r + s] = terms[first_s[8 + r, s]]
+            pick = first_s[8 + r, s]
+            code = pick & 255
+            send_two[SLOT * r + s] = term((pick >> 8) & 255, code >> 3, pick >> 16, code)
     exchange(send_two, recv_two, 1, exists)
+
+    for e in range(LIVE):
+        last = first_s[30, 8 * e]
+        for k in range(6):
+            terms[8 * e + k] = term(e, k, last, first_s[1, 8 * e + k])
+
     settle(send_two, recv_two, 1)
     for r in ROUTES:
-        terms[96 + SLOT * r : 96 + SLOT * (r + 1)] = recv_two[SLOT * r : SLOT * (r + 1)]
+        terms[ARRIVED + SLOT * r : ARRIVED + SLOT * (r + 1)] = recv_two[SLOT * r : SLOT * (r + 1)]
 
     for f in range(27):
         summed = terms[second_s[f, 0]].astype(jnp.float32) + terms[second_s[f, 1]].astype(
@@ -352,16 +421,20 @@
                 pltpu.VMEM((6, 256), jnp.int32),
                 pltpu.VMEM((6, 256), jnp.int32),
                 pltpu.SMEM((1, devices), jnp.int32),
-                pltpu.VMEM((24, 128), jnp.int32),
                 pltpu.VMEM((32, 128), jnp.int32),
-                pltpu.SMEM((24, 128), jnp.int32),
+                pltpu.VMEM((32, 128), jnp.int32),
+                pltpu.SMEM((32, 128), jnp.int32),
                 pltpu.SMEM((32, 128), jnp.int32),
                 pltpu.VMEM((48, 128), jnp.int32),
                 pltpu.VMEM((48, 128), jnp.int32),
-                pltpu.VMEM((47, 16, 128), jnp.bfloat16),
+                pltpu.VMEM((48, 128), jnp.int32),
+                pltpu.VMEM((28, 16, 128), jnp.bfloat16),
                 pltpu.VMEM((faces, functionals, trace), jnp.float32),
                 pltpu.VMEM((LIVE, 16, 768), jnp.bfloat16),
-                pltpu.VMEM((117, 16, 128), jnp.bfloat16),
+                pltpu.VMEM((REMOTE, 16, 256), jnp.bfloat16),
+                pltpu.VMEM((LIVE, 7, 16, 128), jnp.float32),
+                pltpu.VMEM((REMOTE + 1, 7, 16, 128), jnp.float32),
+                pltpu.VMEM((ZERO_ROW + 1, 16, 128), jnp.bfloat16),
                 pltpu.VMEM((20, 16, 128), jnp.bfloat16),
                 pltpu.VMEM((20, 16, 128), jnp.bfloat16),
                 pltpu.VMEM((20, 16, 128), jnp.bfloat16),

time: 20.3 us -> 17.6 us (0.87)
  Pallas kernels: 19.4 us -> 16.8 us
    pallas_call x1, Pallas kernels: 19.4 us -> 16.8 us  [per_device(): pl.pallas_call(functools.partial(kernel, devices), name='sweeps', out_sha...]
where the time goes in v4:
time: 17.6 us; the launch traced here: 17.5 us
  Pallas kernels  16.8 us (95%)
  local copies, waits for them, and re-layouts  0.69 us (4%)
    pallas_call x1, Pallas kernels, per_device(): pl.pallas_call(functools.partial(kernel, devices), name='sweeps', out_sha...  16.8 us
    unnamed x1, local copies, waits for them, and re-layouts  0.69 us

profile of v4, /device:TPU:6, one launch (start us, length us, event | category | flops | bytes accessed | tf_op | source)
XLA Modules:
  0.0 17.5 jit_solution(9121023898448602969)
XLA Ops:
  0.0 16.8 %sweeps.1 = f32[27,16,125]{2,1,0:T(8,128)S(1)} custom-call(bf16[12,750,750]{2,1,0:T(8,128)(2,1)} %mats_hbm.1, bf16[27,125,125]{2,1,0:T(8,128)(2,1)} %blocks_hbm.1, bf16[27,16,125]{2,1,0:T(8,128)(2,1)} %rhs_hbm.1, s32[6,1536]{1,0:T(8,128)} %bitcast.3, s32[6,1536]{1,0:T(8,128)} %bitcast.4, s32[1,128]{1,0:T(1,128)} %bitcast.5), custom_call_target="tpu_custom_call" | custom-call | tf_op jit(solution)/shard_map/sweeps/pallas_call | solution.py:411
  16.8 0.7 %copy.8 = f32[27,16,125]{2,1,0:T(8,128)} copy(f32[27,16,125]{2,1,0:T(8,128)S(1)} %sweeps.1) | data formatting | bytes 432000

commit v5 on v4

--- a/solution.py
+++ b/solution.py
@@ -15,6 +15,9 @@
 ZERO_ROW = 92
 WINDOW = 142
 REMOTE = 16
+PICK_BACK = 80
+PICK_OUT = 84
+QUEUE = 88
 ROUTES = (0, 1, 3, 4)
 PLANE = 32
 MESH = pl.DeviceIdType.MESH
@@ -68,7 +71,7 @@
     return TRACE * side - row_start(side)
 
 
-def index_tables(me, devices, faces, codes, shift, count_of):
+def index_tables(me, devices, right_first, faces, codes, shift, count_of):
     shape = (8, 128)
     row = lax.broadcasted_iota(jnp.int32, shape, 0)
     lane = lax.broadcasted_iota(jnp.int32, shape, 1)
@@ -101,8 +104,12 @@
     sends = (mine_key == device) & (row < 5)
     takes = (key == me) & (row != 2)
     sent = jnp.where(sends & (row != 2), 1, 0)
+    in_first = jnp.where((row > 2) == right_first, sent, 0)
+    firsts = jnp.broadcast_to(jnp.sum(in_first, axis=0, keepdims=True), shape)
     remote = jnp.broadcast_to(jnp.sum(sent, axis=0, keepdims=True), shape)
-    upper = jnp.where(row == 5, remote, jnp.where(sends, 1, 0))
+    seconds = remote - firsts
+    lists = jnp.where(row == 5, firsts, jnp.where(row == 6, seconds, 0))
+    upper = jnp.where(row >= 5, lists, jnp.where(sends, 1, 0))
     both = jnp.concatenate([upper, takes.astype(jnp.int32)], axis=0)
     lane16 = lax.broadcasted_iota(jnp.int32, (16, 128), 1)
     rank = both
@@ -113,53 +120,63 @@
     place = jnp.where(mine_key == me, mine_local, 27)
     side = lane & 7
     code = side * 8 + mine_code
-    order = jnp.broadcast_to(send_rank[5:6, :], shape)
-    slot = jnp.sum(jnp.where(sent > 0, SLOT * row + send_rank, 0), axis=0, keepdims=True)
+    order = jnp.where(
+        firsts > 0,
+        jnp.broadcast_to(send_rank[5:6, :], shape),
+        REMOTE // 2 + jnp.broadcast_to(send_rank[6:7, :], shape),
+    )
+    base = jnp.where(row > 2, SLOT * (row - 3), SLOT * row)
+    slot = jnp.sum(jnp.where(sent > 0, base + send_rank, 0), axis=0, keepdims=True)
     slot = jnp.broadcast_to(slot, shape)
-    inner = remote
+    inner = lists
     for step in (1, 2, 4):
         inner = inner + jnp.where(side >= step, pltpu.roll(inner, step, 1), 0)
-    fields = jnp.where(row == 0, slot, jnp.where(row == 1, code, lane >> 3))
-    fields = jnp.where(row == 3, row_start(side) >> 4, fields)
-    fields = jnp.where(row == 4, row_skew(side), fields)
-    fields = jnp.where(row == 5, jnp.where(inner == remote, 0, 1), fields)
+    earlier = jnp.where(
+        firsts > 0,
+        jnp.broadcast_to(inner[5:6, :], shape),
+        jnp.broadcast_to(inner[6:7, :], shape),
+    )
+    element = lane >> 3
+    adds = jnp.where(earlier == 1, 0, 1)
+    field = slot | (code << 5) | (element << 11) | ((row_start(side) >> 4) << 15)
+    field = field | (row_skew(side) << 21) | (adds << 26)
     queue = jnp.where(remote > 0, order, -1)
-    listed = jnp.zeros(shape, jnp.int32)
-    for q in range(REMOTE):
-        found = jnp.sum(jnp.where(queue == q, fields, 0), axis=1, keepdims=True)
-        listed = jnp.where(lane == q, found, listed)
-    last = jnp.where((side == 7) & (inner > 0), order + remote, 0)
+    last = jnp.where(row == 6, REMOTE // 2, 0) + send_rank
+    last = jnp.where((side == 7) & (inner > 0), last, 0)
     for step in (1, 2, 4):
         last = last + pltpu.roll(last, 128 - step, 1)
-    listed = jnp.where(row == 6, last, listed)
-    head = jnp.where(row == 0, place, code)
-    packed = code | ((lane >> 3) << 8) | (last << 16)
+    last_one = jnp.broadcast_to(last[5:6, :], shape)
+    last_two = jnp.broadcast_to(last[6:7, :], shape)
+    packed = code | (element << 8) | (last_one << 16) | (last_two << 24)
+    first = jnp.where(row == 0, place, packed)
     values = jnp.concatenate([packed, local], axis=0)
     slot_of = jnp.where(both > 0, rank, -1)
-    picks = jnp.zeros((16, 128), jnp.int32)
     for s in range(SLOT):
         found = jnp.sum(jnp.where(slot_of == s, values, 0), axis=1, keepdims=True)
-        picks = jnp.where(lane16 == s, found, picks)
-    first = jnp.concatenate([head, picks, listed], axis=0)
+        first = jnp.where(lane == PICK_OUT + s, found[:8], first)
+        first = jnp.where(lane == PICK_BACK + s, found[8:], first)
+    for t in range(2):
+        found = jnp.sum(jnp.where(queue == row + 8 * t, field, 0), axis=1, keepdims=True)
+        first = jnp.where(lane == QUEUE + t, found, first)
 
     home = jnp.where(mine_key == me, local, -1)
     match = jnp.where(row == 2, home, jnp.where(takes, local, -1))
     source = jnp.where(row == 2, lane, ARRIVED + SLOT * row + take_rank)
-    tall = (32, 128)
-    own = lax.broadcasted_iota(jnp.int32, tall, 0)
-    lane32 = lax.broadcasted_iota(jnp.int32, tall, 1)
-    most = jnp.full(tall, -1, jnp.int32)
-    least = jnp.full(tall, 999, jnp.int32)
-    for r in range(5):
-        same = jnp.broadcast_to(match[r : r + 1, :], tall) == own
-        value = jnp.broadcast_to(source[r : r + 1, :], tall)
-        most = jnp.maximum(most, jnp.where(same, value, -1))
-        least = jnp.minimum(least, jnp.where(same, value, 999))
-    most = jnp.max(most, axis=1, keepdims=True)
-    least = jnp.min(least, axis=1, keepdims=True)
-    one = jnp.where(most < 0, ZERO_ROW, most)
-    two = jnp.where(least >= most, ZERO_ROW, least)
-    second = jnp.where(lane32 == 0, one, jnp.where(lane32 == 1, two, 0))
+    second = jnp.zeros(shape, jnp.int32)
+    for t in range(4):
+        own = row + 8 * t
+        most = jnp.full(shape, -1, jnp.int32)
+        least = jnp.full(shape, 999, jnp.int32)
+        for r in range(5):
+            same = jnp.broadcast_to(match[r : r + 1, :], shape) == own
+            value = jnp.broadcast_to(source[r : r + 1, :], shape)
+            most = jnp.maximum(most, jnp.where(same, value, -1))
+            least = jnp.minimum(least, jnp.where(same, value, 999))
+        most = jnp.max(most, axis=1, keepdims=True)
+        least = jnp.min(least, axis=1, keepdims=True)
+        one = jnp.where(most < 0, ZERO_ROW, most)
+        two = jnp.where(least >= most, ZERO_ROW, least)
+        second = jnp.where(lane == 2 * t, one, jnp.where(lane == 2 * t + 1, two, second))
     return first, second
 
 
@@ -170,9 +187,28 @@
     mats, blocks, rhs, faces, codes, counts,
     first_v, second_v, first_s, second_s, forward, backward, skewed,
     table, solved, frames, shifted, home, sums, terms, send_one, recv_one, send_two, recv_two,
-    relay, mat_sem, load_sem, send_sem, recv_sem, relay_sem,
+    relay, held_one, held_two, mat_sem, load_sem, send_sem, recv_sem, relay_sem,
 ):
     me = lax.axis_index("elem")
+    barrier = pltpu.get_barrier_semaphore()
+
+    def greet(signals):
+        for wanted, peer in signals:
+
+            @pl.when(wanted)
+            def _(peer=peer):
+                pl.semaphore_signal(
+                    barrier, inc=1, device_id=(peer,), device_id_type=MESH
+                )
+
+    place = lax.rem(me, PLANE)
+    late = (place >= PLANE - 2) & (me < devices - PLANE)
+    late_one = (place == PLANE - 1) & (me < devices - PLANE)
+    early = (place < 2) & (me >= PLANE)
+    early_zero = (place == 0) & (me >= PLANE)
+    relays = (place >= PLANE - 8) & (place < PLANE - 6) & (me < devices - PLANE)
+    relays_zero = (place == PLANE - 8) & (me < devices - PLANE)
+    greet([(relays, me + 8), (late, me - 6), (late_one, me - 7)])
     start = 12 * me - 24
     base = pl.multiple_of(jnp.clip((start // 128) * 128, 0, faces_hbm.shape[1] - 256), 128)
     shift = (256 - (start - base)) % 256
@@ -186,38 +222,22 @@
     ]
     for load in loads:
         load.start()
-    barrier = pltpu.get_barrier_semaphore()
     peers = [me + (r - 2) for r in range(5)]
     exists = [(me >= 2 - r) if r < 2 else (me < devices + 2 - r) for r in range(5)]
-    place = lax.rem(me, PLANE)
-    late = (place >= PLANE - 2) & (me < devices - PLANE)
-    late_one = (place == PLANE - 1) & (me < devices - PLANE)
-    early = (place < 2) & (me >= PLANE)
-    early_zero = (place == 0) & (me >= PLANE)
-    relays = (place >= PLANE - 8) & (place < PLANE - 6) & (me < devices - PLANE)
-    relays_zero = (place == PLANE - 8) & (me < devices - PLANE)
     greets = list(exists)
     greets[3] = exists[3] & jnp.logical_not(late_one)
     greets[4] = exists[4] & jnp.logical_not(late)
     direct = list(exists)
     direct[0] = exists[0] & jnp.logical_not(early)
     direct[1] = exists[1] & jnp.logical_not(early_zero)
-    signals = [(greets[r], peers[r]) for r in ROUTES]
-    signals += [(late, me - 6), (late_one, me - 7), (relays, me + 8)]
-    for wanted, peer in signals:
-
-        @pl.when(wanted)
-        def _(peer=peer):
-            pl.semaphore_signal(barrier, inc=1, device_id=(peer,), device_id_type=MESH)
-
+    right_first = lax.rem(me // 2, 4) == 0
+    greet([(greets[r], peers[r]) for r in ROUTES])
     heard = 4 - jnp.maximum(2 - me, 0) - jnp.maximum(me - (devices - 3), 0)
     heard = heard - early_zero.astype(jnp.int32)
     heard = heard + relays.astype(jnp.int32) + relays_zero.astype(jnp.int32)
     mat_loads = [
         pltpu.make_async_copy(mats_hbm.at[e], mats.at[e], mat_sem.at[e]) for e in range(LIVE)
     ]
-    for load in mat_loads:
-        load.start()
 
     table[...] = jnp.zeros_like(table)
     terms[...] = jnp.zeros_like(terms)
@@ -226,9 +246,11 @@
 
     for load in loads[:3]:
         load.wait()
+    for load in mat_loads:
+        load.start()
     count_of = [counts[0, jnp.clip(me - 2 + r, 0, devices - 1)] for r in range(5)]
     first_v[...], second_v[...] = index_tables(
-        me, devices, faces[...], codes[...], shift, count_of
+        me, devices, right_first, faces[...], codes[...], shift, count_of
     )
     tables = [
         pltpu.make_async_copy(first_v, first_s, load_sem.at[5]),
@@ -291,16 +313,16 @@
             def _(r=r):
                 act(r)
 
-    def settle(send, recv, leg):
-        for r in ROUTES:
-
-            @pl.when(exists[r])
+    def settle(send, recv, leg, routes, wanted=True):
+        for r in routes:
+
+            @pl.when(exists[r] & wanted)
             def _(r=r):
                 route(send, recv, leg, r, r).wait_recv()
 
     for r in ROUTES:
         for s in range(SLOT):
-            send_one[SLOT * r + s] = table[first_s[16 + r, s]]
+            send_one[SLOT * r + s] = table[first_s[r, PICK_BACK + s]]
     pl.semaphore_wait(barrier, heard)
     when_each((early, early_zero), lambda r: to_relay(r).start())
     exchange(send_one, recv_one, 0, direct)
@@ -319,7 +341,7 @@
         pieces = []
         for k in range(6):
             value = table[first_s[0, 8 * e + k]].astype(jnp.float32)
-            pieces.append(turned(value, forward, first_s[1, 8 * e + k]))
+            pieces.append(turned(value, forward, first_s[1, 8 * e + k] & 255))
         pieces.append(jnp.zeros((16, 128), jnp.float32))
         for c in range(6):
             column = jnp.where(lane < TRACE - 3 * c, pieces[c], pieces[c + 1])
@@ -340,52 +362,65 @@
     when_each((relays, relays_zero), forward_on)
     lax.fori_loop(5, LIVE, apply, 0)
 
-    settle(send_one, recv_one, 0)
     total = None
     for q in range(REMOTE):
-        slot, code, e, start_row, skew, adds = [first_s[24 + i, q] for i in range(6)]
-        value = turned(recv_one[slot].astype(jnp.float32), skewed, code)
+        if q == 0:
+            settle(send_one, recv_one, 0, (3, 4), right_first)
+            settle(send_one, recv_one, 0, (0, 1), jnp.logical_not(right_first))
+            held_one[...] = recv_one[pl.ds(jnp.where(right_first, 12, 0), 8)]
+        if q == REMOTE // 2:
+            settle(send_one, recv_one, 0, (0, 1), right_first)
+            settle(send_one, recv_one, 0, (3, 4), jnp.logical_not(right_first))
+            held_two[...] = recv_one[pl.ds(jnp.where(right_first, 0, 12), 8)]
+            total = None
+        word = first_s[q % 8, QUEUE + q // 8]
+        held = held_one if q < REMOTE // 2 else held_two
+        skew = (word >> 21) & 31
+        value = held[word & 31].astype(jnp.float32)
+        value = turned(value, skewed, (word >> 5) & 63)
         node = lane - skew
         main = jnp.where((node >= 0) & (node < TRACE), value, 0.0)
         rest = jnp.where(lane <= skew - 4, value, 0.0)
         shifted[q, :, :128] = main.astype(jnp.bfloat16)
         shifted[q, :, 128:] = rest.astype(jnp.bfloat16)
-        rows = pl.ds(start_row * 16, WINDOW)
+        rows = pl.ds(((word >> 15) & 63) * 16, WINDOW)
         part = jnp.dot(
-            shifted[q, :, :WINDOW], mats[e, rows, :], preferred_element_type=jnp.float32
-        )
-        total = part if total is None else part + total * adds.astype(jnp.float32)
+            shifted[q, :, :WINDOW],
+            mats[(word >> 11) & 15, rows, :],
+            preferred_element_type=jnp.float32,
+        )
+        adds = (word >> 26).astype(jnp.float32)
+        total = part if total is None else part + total * adds
         columns(sums, q + 1, total)
 
-    def term(e, k, last, code):
+    def term(word):
+        code, e = word & 255, (word >> 8) & 255
+        one, two = (word >> 16) & 255, word >> 24
+        k = code >> 3
         value = jnp.where(
             lane < TRACE - 3 * k,
-            home[e, k + 1] + sums[last, k + 1],
-            home[e, k] + sums[last, k],
+            home[e, k + 1] + (sums[one, k + 1] + sums[two, k + 1]),
+            home[e, k] + (sums[one, k] + sums[two, k]),
         )
         value = value.astype(jnp.bfloat16).astype(jnp.float32)
         return turned(value, backward, code).astype(jnp.bfloat16)
 
     for r in ROUTES:
         for s in range(SLOT):
-            pick = first_s[8 + r, s]
-            code = pick & 255
-            send_two[SLOT * r + s] = term((pick >> 8) & 255, code >> 3, pick >> 16, code)
+            send_two[SLOT * r + s] = term(first_s[r, PICK_OUT + s])
     exchange(send_two, recv_two, 1, exists)
 
     for e in range(LIVE):
-        last = first_s[30, 8 * e]
         for k in range(6):
-            terms[8 * e + k] = term(e, k, last, first_s[1, 8 * e + k])
-
-    settle(send_two, recv_two, 1)
+            terms[8 * e + k] = term(first_s[1, 8 * e + k])
+
+    settle(send_two, recv_two, 1, ROUTES)
     for r in ROUTES:
         terms[ARRIVED + SLOT * r : ARRIVED + SLOT * (r + 1)] = recv_two[SLOT * r : SLOT * (r + 1)]
 
     for f in range(27):
-        summed = terms[second_s[f, 0]].astype(jnp.float32) + terms[second_s[f, 1]].astype(
-            jnp.float32
-        )
+        one, two = second_s[f % 8, 2 * (f // 8)], second_s[f % 8, 2 * (f // 8) + 1]
+        summed = terms[one].astype(jnp.float32) + terms[two].astype(jnp.float32)
         residual = (rhs[f].astype(jnp.float32) - summed[:, :TRACE]).astype(jnp.bfloat16)
         out_ref[f] = solved[f] + jnp.dot(
             residual, blocks[f], preferred_element_type=jnp.float32
@@ -421,10 +456,10 @@
                 pltpu.VMEM((6, 256), jnp.int32),
                 pltpu.VMEM((6, 256), jnp.int32),
                 pltpu.SMEM((1, devices), jnp.int32),
-                pltpu.VMEM((32, 128), jnp.int32),
-                pltpu.VMEM((32, 128), jnp.int32),
-                pltpu.SMEM((32, 128), jnp.int32),
-                pltpu.SMEM((32, 128), jnp.int32),
+                pltpu.VMEM((8, 128), jnp.int32),
+                pltpu.VMEM((8, 128), jnp.int32),
+                pltpu.SMEM((8, 128), jnp.int32),
+                pltpu.SMEM((8, 128), jnp.int32),
                 pltpu.VMEM((48, 128), jnp.int32),
                 pltpu.VMEM((48, 128), jnp.int32),
                 pltpu.VMEM((48, 128), jnp.int32),
@@ -440,6 +475,8 @@
                 pltpu.VMEM((20, 16, 128), jnp.bfloat16),
                 pltpu.VMEM((20, 16, 128), jnp.bfloat16),
                 pltpu.VMEM((8, 16, 128), jnp.bfloat16),
+                pltpu.VMEM((8, 16, 128), jnp.bfloat16),
+                pltpu.VMEM((8, 16, 128), jnp.bfloat16),
                 pltpu.SemaphoreType.DMA((LIVE,)),
                 pltpu.SemaphoreType.DMA((7,)),
                 pltpu.SemaphoreType.DMA((2, 5)),

time: 17.6 us -> 17.4 us (0.989)
  Pallas kernels: 16.8 us -> 16.6 us
    pallas_call x1, Pallas kernels: 16.8 us -> 16.6 us  [per_device(): pl.pallas_call(functools.partial(kernel, devices), name='sweeps', out_sha...]
where the time goes in v5:
time: 17.4 us; the launch traced here: 17.2 us
  Pallas kernels  16.6 us (95%)
  local copies, waits for them, and re-layouts  0.69 us (4%)
    pallas_call x1, Pallas kernels, per_device(): pl.pallas_call(functools.partial(kernel, devices), name='sweeps', out_sha...  16.6 us
    unnamed x1, local copies, waits for them, and re-layouts  0.69 us

profile of v5, /device:TPU:6, one launch (start us, length us, event | category | flops | bytes accessed | tf_op | source)
XLA Modules:
  0.0 17.2 jit_solution(7895490358287245554)
XLA Ops:
  0.0 16.6 %sweeps.1 = f32[27,16,125]{2,1,0:T(8,128)S(1)} custom-call(bf16[12,750,750]{2,1,0:T(8,128)(2,1)} %mats_hbm.1, bf16[27,125,125]{2,1,0:T(8,128)(2,1)} %blocks_hbm.1, bf16[27,16,125]{2,1,0:T(8,128)(2,1)} %rhs_hbm.1, s32[6,1536]{1,0:T(8,128)} %bitcast.3, s32[6,1536]{1,0:T(8,128)} %bitcast.4, s32[1,128]{1,0:T(1,128)} %bitcast.5), custom_call_target="tpu_custom_call" | custom-call | tf_op jit(solution)/shard_map/sweeps/pallas_call | solution.py:446
  16.6 0.7 %copy.8 = f32[27,16,125]{2,1,0:T(8,128)} copy(f32[27,16,125]{2,1,0:T(8,128)S(1)} %sweeps.1) | data formatting | bytes 432000

commit v6 on v5

--- a/solution.py
+++ b/solution.py
@@ -19,6 +19,7 @@
 PICK_OUT = 84
 QUEUE = 88
 ROUTES = (0, 1, 3, 4)
+SEMS = (0, 1, None, 2, 3)
 PLANE = 32
 MESH = pl.DeviceIdType.MESH
 
@@ -187,7 +188,7 @@
     mats, blocks, rhs, faces, codes, counts,
     first_v, second_v, first_s, second_s, forward, backward, skewed,
     table, solved, frames, shifted, home, sums, terms, send_one, recv_one, send_two, recv_two,
-    relay, held_one, held_two, mat_sem, load_sem, send_sem, recv_sem, relay_sem,
+    relay, held_one, held_two, pairs, load_sem, send_sem, recv_sem, relay_sem,
 ):
     me = lax.axis_index("elem")
     barrier = pltpu.get_barrier_semaphore()
@@ -236,11 +237,15 @@
     heard = heard - early_zero.astype(jnp.int32)
     heard = heard + relays.astype(jnp.int32) + relays_zero.astype(jnp.int32)
     mat_loads = [
-        pltpu.make_async_copy(mats_hbm.at[e], mats.at[e], mat_sem.at[e]) for e in range(LIVE)
+        pltpu.make_async_copy(
+            mats_hbm.at[pl.ds(3 * c, 3)], mats.at[pl.ds(3 * c, 3)], load_sem.at[c]
+        )
+        for c in range(3)
     ]
 
     table[...] = jnp.zeros_like(table)
     terms[...] = jnp.zeros_like(terms)
+    pairs[...] = jnp.zeros_like(pairs)
     sums[0] = jnp.zeros_like(sums[0])
     forward[...], backward[...], skewed[...] = code_tables()
 
@@ -254,33 +259,32 @@
     )
     tables = [
         pltpu.make_async_copy(first_v, first_s, load_sem.at[5]),
-        pltpu.make_async_copy(second_v, second_s, load_sem.at[6]),
+        pltpu.make_async_copy(second_v, second_s, load_sem.at[3]),
     ]
-    for copy in tables:
-        copy.start()
+    tables[0].start()
 
     loads[3].wait()
+    tables[1].start()
     loads[4].wait()
     for f in range(27):
         value = jnp.dot(rhs[f], blocks[f], preferred_element_type=jnp.float32)
         solved[f] = value
         table[f, :, :TRACE] = value.astype(jnp.bfloat16)
 
-    for copy in tables:
-        copy.wait()
+    tables[0].wait()
 
     def route(send, recv, leg, r, slot):
         return pltpu.make_async_remote_copy(
             src_ref=send.at[pl.ds(SLOT * r, SLOT)],
             dst_ref=recv.at[pl.ds(SLOT * slot, SLOT)],
-            send_sem=send_sem.at[leg, r],
-            recv_sem=recv_sem.at[leg, slot],
+            send_sem=send_sem.at[SEMS[r]],
+            recv_sem=recv_sem.at[leg, SEMS[slot]],
             device_id=(peers[r],),
             device_id_type=MESH,
         )
 
-    def exchange(send, recv, leg, sends):
-        for r in ROUTES:
+    def exchange(send, recv, leg, sends, routes=ROUTES):
+        for r in routes:
 
             @pl.when(sends[r])
             def _(r=r):
@@ -290,8 +294,8 @@
         return pltpu.make_async_remote_copy(
             src_ref=send_one.at[pl.ds(SLOT * r, SLOT)],
             dst_ref=relay.at[pl.ds(SLOT * r, SLOT)],
-            send_sem=relay_sem.at[0, r],
-            recv_sem=relay_sem.at[1, r],
+            send_sem=send_sem.at[r],
+            recv_sem=relay_sem.at[r],
             device_id=(me - 8,),
             device_id_type=MESH,
         )
@@ -300,8 +304,8 @@
         return pltpu.make_async_remote_copy(
             src_ref=relay.at[pl.ds(SLOT * r, SLOT)],
             dst_ref=recv_one.at[pl.ds(SLOT * (4 - r), SLOT)],
-            send_sem=relay_sem.at[2, r],
-            recv_sem=recv_sem.at[0, 4 - r],
+            send_sem=load_sem.at[3 + r],
+            recv_sem=recv_sem.at[0, SEMS[4 - r]],
             device_id=(me + 6 + r,),
             device_id_type=MESH,
         )
@@ -326,6 +330,7 @@
     pl.semaphore_wait(barrier, heard)
     when_each((early, early_zero), lambda r: to_relay(r).start())
     exchange(send_one, recv_one, 0, direct)
+    tables[1].wait()
 
     def forward_on(r):
         to_relay(r).wait_recv()
@@ -353,14 +358,25 @@
         ref[at, 6, :, :110] = value[:, 640:750]
 
     def apply(e, carry):
-        pltpu.make_async_copy(mats_hbm.at[e], mats.at[e], mat_sem.at[e]).wait()
         value = jnp.dot(frames[e, :, :750], mats[e], preferred_element_type=jnp.float32)
         columns(home, e, value)
         return carry
 
-    lax.fori_loop(0, 5, apply, 0)
+    mat_loads[0].wait()
+    lax.fori_loop(0, 3, apply, 0)
+    mat_loads[1].wait()
+    lax.fori_loop(3, 4, apply, 0)
     when_each((relays, relays_zero), forward_on)
-    lax.fori_loop(5, LIVE, apply, 0)
+    lax.fori_loop(4, 6, apply, 0)
+    mat_loads[2].wait()
+    lax.fori_loop(6, LIVE, apply, 0)
+
+    when_each((early, early_zero), lambda r: to_relay(r).wait_send())
+    for r in ROUTES:
+
+        @pl.when(direct[r])
+        def _(r=r):
+            route(send_one, recv_one, 0, r, 4 - r).wait_send()
 
     total = None
     for q in range(REMOTE):
@@ -405,33 +421,43 @@
         value = value.astype(jnp.bfloat16).astype(jnp.float32)
         return turned(value, backward, code).astype(jnp.bfloat16)
 
-    for r in ROUTES:
+    def partials(r):
         for s in range(SLOT):
             send_two[SLOT * r + s] = term(first_s[r, PICK_OUT + s])
-    exchange(send_two, recv_two, 1, exists)
+
+    for r in (4, 3, 1):
+        partials(r)
+    exchange(send_two, recv_two, 1, exists, (4, 3))
+    partials(0)
+    exchange(send_two, recv_two, 1, exists, (1, 0))
 
     for e in range(LIVE):
         for k in range(6):
             terms[8 * e + k] = term(first_s[1, 8 * e + k])
 
+    for f in range(26):
+        column = 128 * (f % 2)
+        pairs[f // 2, :, column : column + TRACE] = blocks[f]
+
     settle(send_two, recv_two, 1, ROUTES)
     for r in ROUTES:
         terms[ARRIVED + SLOT * r : ARRIVED + SLOT * (r + 1)] = recv_two[SLOT * r : SLOT * (r + 1)]
 
-    for f in range(27):
+    def residual(f):
         one, two = second_s[f % 8, 2 * (f // 8)], second_s[f % 8, 2 * (f // 8) + 1]
         summed = terms[one].astype(jnp.float32) + terms[two].astype(jnp.float32)
-        residual = (rhs[f].astype(jnp.float32) - summed[:, :TRACE]).astype(jnp.bfloat16)
-        out_ref[f] = solved[f] + jnp.dot(
-            residual, blocks[f], preferred_element_type=jnp.float32
-        )
-    when_each((early, early_zero), lambda r: to_relay(r).wait_send())
+        return (rhs[f].astype(jnp.float32) - summed[:, :TRACE]).astype(jnp.bfloat16)
+
+    for f in range(0, 26, 2):
+        both = jnp.concatenate([residual(f), residual(f + 1)], axis=0)
+        step = jnp.dot(both, pairs[f // 2], preferred_element_type=jnp.float32)
+        out_ref[f] = solved[f] + step[:16, :TRACE]
+        out_ref[f + 1] = solved[f + 1] + step[16:, 128 : 128 + TRACE]
+    out_ref[26] = solved[26] + jnp.dot(
+        residual(26), blocks[26], preferred_element_type=jnp.float32
+    )
     when_each((relays, relays_zero), lambda r: onward(r).wait_send())
     for r in ROUTES:
-
-        @pl.when(direct[r])
-        def _(r=r):
-            route(send_one, recv_one, 0, r, 4 - r).wait_send()
 
         @pl.when(exists[r])
         def _(r=r):
@@ -477,11 +503,11 @@
                 pltpu.VMEM((8, 16, 128), jnp.bfloat16),
                 pltpu.VMEM((8, 16, 128), jnp.bfloat16),
                 pltpu.VMEM((8, 16, 128), jnp.bfloat16),
-                pltpu.SemaphoreType.DMA((LIVE,)),
-                pltpu.SemaphoreType.DMA((7,)),
-                pltpu.SemaphoreType.DMA((2, 5)),
-                pltpu.SemaphoreType.DMA((2, 5)),
-                pltpu.SemaphoreType.DMA((3, 2)),
+                pltpu.VMEM((13, trace, 256), jnp.bfloat16),
+                pltpu.SemaphoreType.DMA((6,)),
+                pltpu.SemaphoreType.DMA((4,)),
+                pltpu.SemaphoreType.DMA((2, 4)),
+                pltpu.SemaphoreType.DMA((2,)),
             ],
             compiler_params=pltpu.CompilerParams(collective_id=0, has_side_effects=True),
         )(elem_mats, face_blocks, rhs, elem_faces.T, orient.T, counts.reshape(1, -1))

time: 17.4 us -> 17 us (0.977)
  Pallas kernels: 16.6 us -> 16.2 us
    pallas_call x1, Pallas kernels: 16.6 us -> 16.2 us  [per_device(): pl.pallas_call(functools.partial(kernel, devices), name='sweeps', out_sha...]
where the time goes in v6:
time: 17 us; the launch traced here: 16.9 us
  Pallas kernels  16.2 us (95%)
  local copies, waits for them, and re-layouts  0.69 us (4%)
    pallas_call x1, Pallas kernels, per_device(): pl.pallas_call(functools.partial(kernel, devices), name='sweeps', out_sha...  16.2 us
    unnamed x1, local copies, waits for them, and re-layouts  0.69 us

profile of v6, /device:TPU:6, one launch (start us, length us, event | category | flops | bytes accessed | tf_op | source)
XLA Modules:
  0.0 16.9 jit_solution(7029236573952497855)
XLA Ops:
  0.0 16.2 %sweeps.1 = f32[27,16,125]{2,1,0:T(8,128)S(1)} custom-call(bf16[12,750,750]{2,1,0:T(8,128)(2,1)} %mats_hbm.1, bf16[27,125,125]{2,1,0:T(8,128)(2,1)} %blocks_hbm.1, bf16[27,16,125]{2,1,0:T(8,128)(2,1)} %rhs_hbm.1, s32[6,1536]{1,0:T(8,128)} %bitcast.3, s32[6,1536]{1,0:T(8,128)} %bitcast.4, s32[1,128]{1,0:T(1,128)} %bitcast.5), custom_call_target="tpu_custom_call" | custom-call | tf_op jit(solution)/shard_map/sweeps/pallas_call | solution.py:472
  16.2 0.7 %copy.8 = f32[27,16,125]{2,1,0:T(8,128)} copy(f32[27,16,125]{2,1,0:T(8,128)S(1)} %sweeps.1) | data formatting | bytes 432000

commit v7 on v6

--- a/solution.py
+++ b/solution.py
@@ -207,9 +207,9 @@
     late_one = (place == PLANE - 1) & (me < devices - PLANE)
     early = (place < 2) & (me >= PLANE)
     early_zero = (place == 0) & (me >= PLANE)
-    relays = (place >= PLANE - 8) & (place < PLANE - 6) & (me < devices - PLANE)
-    relays_zero = (place == PLANE - 8) & (me < devices - PLANE)
-    greet([(relays, me + 8), (late, me - 6), (late_one, me - 7)])
+    relays = (place >= PLANE - 8) & (place < PLANE - 6) & (me >= PLANE)
+    relays_zero = (place == PLANE - 8) & (me >= PLANE)
+    greet([(relays, me - 24), (late, me + 26), (late_one, me + 25)])
     start = 12 * me - 24
     base = pl.multiple_of(jnp.clip((start // 128) * 128, 0, faces_hbm.shape[1] - 256), 128)
     shift = (256 - (start - base)) % 256
@@ -296,7 +296,7 @@
             dst_ref=relay.at[pl.ds(SLOT * r, SLOT)],
             send_sem=send_sem.at[r],
             recv_sem=relay_sem.at[r],
-            device_id=(me - 8,),
+            device_id=(me + 24,),
             device_id_type=MESH,
         )
 
@@ -306,7 +306,7 @@
             dst_ref=recv_one.at[pl.ds(SLOT * (4 - r), SLOT)],
             send_sem=load_sem.at[3 + r],
             recv_sem=recv_sem.at[0, SEMS[4 - r]],
-            device_id=(me + 6 + r,),
+            device_id=(me - 26 + r,),
             device_id_type=MESH,
         )
 
@@ -362,11 +362,11 @@
         columns(home, e, value)
         return carry
 
+    when_each((relays, relays_zero), forward_on)
     mat_loads[0].wait()
     lax.fori_loop(0, 3, apply, 0)
     mat_loads[1].wait()
     lax.fori_loop(3, 4, apply, 0)
-    when_each((relays, relays_zero), forward_on)
     lax.fori_loop(4, 6, apply, 0)
     mat_loads[2].wait()
     lax.fori_loop(6, LIVE, apply, 0)

time: 17 us -> 16.8 us (0.988)
  Pallas kernels: 16.2 us -> 15.9 us
    pallas_call x1, Pallas kernels: 16.2 us -> 15.9 us  [per_device(): pl.pallas_call(functools.partial(kernel, devices), name='sweeps', out_sha...]
where the time goes in v7:
time: 16.8 us; the launch traced here: 16.6 us
  Pallas kernels  15.9 us (95%)
  local copies, waits for them, and re-layouts  0.69 us (4%)
    pallas_call x1, Pallas kernels, per_device(): pl.pallas_call(functools.partial(kernel, devices), name='sweeps', out_sha...  15.9 us
    unnamed x1, local copies, waits for them, and re-layouts  0.69 us

profile of v7, /device:TPU:6, one launch (start us, length us, event | category | flops | bytes accessed | tf_op | source)
XLA Modules:
  0.0 16.6 jit_solution(13895348309899930993)
XLA Ops:
  0.0 15.9 %sweeps.1 = f32[27,16,125]{2,1,0:T(8,128)S(1)} custom-call(bf16[12,750,750]{2,1,0:T(8,128)(2,1)} %mats_hbm.1, bf16[27,125,125]{2,1,0:T(8,128)(2,1)} %blocks_hbm.1, bf16[27,16,125]{2,1,0:T(8,128)(2,1)} %rhs_hbm.1, s32[6,1536]{1,0:T(8,128)} %bitcast.3, s32[6,1536]{1,0:T(8,128)} %bitcast.4, s32[1,128]{1,0:T(1,128)} %bitcast.5), custom_call_target="tpu_custom_call" | custom-call | tf_op jit(solution)/shard_map/sweeps/pallas_call | solution.py:472
  15.9 0.7 %copy.8 = f32[27,16,125]{2,1,0:T(8,128)} copy(f32[27,16,125]{2,1,0:T(8,128)S(1)} %sweeps.1) | data formatting | bytes 432000

commit v8 on v7

--- a/solution.py
+++ b/solution.py
@@ -425,10 +425,11 @@
         for s in range(SLOT):
             send_two[SLOT * r + s] = term(first_s[r, PICK_OUT + s])
 
-    for r in (4, 3, 1):
+    for r in (4, 3):
         partials(r)
     exchange(send_two, recv_two, 1, exists, (4, 3))
-    partials(0)
+    for r in (1, 0):
+        partials(r)
     exchange(send_two, recv_two, 1, exists, (1, 0))
 
     for e in range(LIVE):
@@ -439,9 +440,13 @@
         column = 128 * (f % 2)
         pairs[f // 2, :, column : column + TRACE] = blocks[f]
 
-    settle(send_two, recv_two, 1, ROUTES)
-    for r in ROUTES:
-        terms[ARRIVED + SLOT * r : ARRIVED + SLOT * (r + 1)] = recv_two[SLOT * r : SLOT * (r + 1)]
+    when_each((relays, relays_zero), lambda r: onward(r).wait_send())
+    for side in ((4, 3), (1, 0)):
+        settle(send_two, recv_two, 1, side)
+        for r in side:
+            terms[ARRIVED + SLOT * r : ARRIVED + SLOT * (r + 1)] = recv_two[
+                SLOT * r : SLOT * (r + 1)
+            ]
 
     def residual(f):
         one, two = second_s[f % 8, 2 * (f // 8)], second_s[f % 8, 2 * (f // 8) + 1]
@@ -456,7 +461,6 @@
     out_ref[26] = solved[26] + jnp.dot(
         residual(26), blocks[26], preferred_element_type=jnp.float32
     )
-    when_each((relays, relays_zero), lambda r: onward(r).wait_send())
     for r in ROUTES:
 
         @pl.when(exists[r])

time: 16.8 us -> 16.7 us (level)
  no operation moved by 1% of the time
where the time goes in v8:
time: 16.7 us; the launch traced here: 16.6 us
  Pallas kernels  15.9 us (95%)
  local copies, waits for them, and re-layouts  0.69 us (4%)
    pallas_call x1, Pallas kernels, per_device(): pl.pallas_call(functools.partial(kernel, devices), name='sweeps', out_sha...  15.9 us
    unnamed x1, local copies, waits for them, and re-layouts  0.69 us

profile of v8, /device:TPU:6, one launch (start us, length us, event | category | flops | bytes accessed | tf_op | source)
XLA Modules:
  0.0 16.6 jit_solution(10543045275097639360)
XLA Ops:
  0.0 15.9 %sweeps.1 = f32[27,16,125]{2,1,0:T(8,128)S(1)} custom-call(bf16[12,750,750]{2,1,0:T(8,128)(2,1)} %mats_hbm.1, bf16[27,125,125]{2,1,0:T(8,128)(2,1)} %blocks_hbm.1, bf16[27,16,125]{2,1,0:T(8,128)(2,1)} %rhs_hbm.1, s32[6,1536]{1,0:T(8,128)} %bitcast.3, s32[6,1536]{1,0:T(8,128)} %bitcast.4, s32[1,128]{1,0:T(1,128)} %bitcast.5), custom_call_target="tpu_custom_call" | custom-call | tf_op jit(solution)/shard_map/sweeps/pallas_call | solution.py:476
  15.9 0.7 %copy.8 = f32[27,16,125]{2,1,0:T(8,128)} copy(f32[27,16,125]{2,1,0:T(8,128)S(1)} %sweeps.1) | data formatting | bytes 432000

commit v9 on v7

--- a/solution.py
+++ b/solution.py
@@ -251,8 +251,6 @@
 
     for load in loads[:3]:
         load.wait()
-    for load in mat_loads:
-        load.start()
     count_of = [counts[0, jnp.clip(me - 2 + r, 0, devices - 1)] for r in range(5)]
     first_v[...], second_v[...] = index_tables(
         me, devices, right_first, faces[...], codes[...], shift, count_of
@@ -262,6 +260,8 @@
         pltpu.make_async_copy(second_v, second_s, load_sem.at[3]),
     ]
     tables[0].start()
+    for load in mat_loads:
+        load.start()
 
     loads[3].wait()
     tables[1].start()

time: 16.8 us -> 17.3 us (1.030)
  Pallas kernels: 15.9 us -> 16.5 us
    pallas_call x1, Pallas kernels: 15.9 us -> 16.5 us  [per_device(): pl.pallas_call(functools.partial(kernel, devices), name='sweeps', out_sha...]
where the time goes in v9:
time: 17.3 us; the launch traced here: 17.2 us
  Pallas kernels  16.5 us (95%)
  local copies, waits for them, and re-layouts  0.69 us (4%)
    pallas_call x1, Pallas kernels, per_device(): pl.pallas_call(functools.partial(kernel, devices), name='sweeps', out_sha...  16.5 us
    unnamed x1, local copies, waits for them, and re-layouts  0.69 us

profile of v9, /device:TPU:6, one launch (start us, length us, event | category | flops | bytes accessed | tf_op | source)
XLA Modules:
  0.0 17.2 jit_solution(11942316746757525641)
XLA Ops:
  0.0 16.5 %sweeps.1 = f32[27,16,125]{2,1,0:T(8,128)S(1)} custom-call(bf16[12,750,750]{2,1,0:T(8,128)(2,1)} %mats_hbm.1, bf16[27,125,125]{2,1,0:T(8,128)(2,1)} %blocks_hbm.1, bf16[27,16,125]{2,1,0:T(8,128)(2,1)} %rhs_hbm.1, s32[6,1536]{1,0:T(8,128)} %bitcast.3, s32[6,1536]{1,0:T(8,128)} %bitcast.4, s32[1,128]{1,0:T(1,128)} %bitcast.5), custom_call_target="tpu_custom_call" | custom-call | tf_op jit(solution)/shard_map/sweeps/pallas_call | solution.py:472
  16.5 0.7 %copy.8 = f32[27,16,125]{2,1,0:T(8,128)} copy(f32[27,16,125]{2,1,0:T(8,128)S(1)} %sweeps.1) | data formatting | bytes 432000
